TPU v7x, 128 devices: a whole 4x4x4 slice. The times are simulated.
128 devices in a mesh: gx: 16 (over z, y_hi, core), gy: 8 (over y_lo, x).
Axes of the slice: x: 4, y: 4 (y_hi: 2, y_lo: 2; y = y_hi * 2 + y_lo), z: 4, core: 2. Of those that a mesh axis runs over, the one named last changes fastest.
Arguments:
- temp_fluid: float32 [256, 512, 1024], P('gx', 'gy'), may hold values from -6 to 6
- velocity: bfloat16 [3, 256, 512, 1024], P(None, 'gx', 'gy'), may hold values from -1 to 1
- wall_old: float32 [256, 512, 128], P('gx', 'gy'), may hold values from -6 to 6
- wall_mask: int32 [256, 512, 128], P('gx', 'gy'), may hold values 0 or 1
- owner_map: int32 [128, 1024, 1], P(('gx', 'gy')), may hold values from 0 to 127; in each aligned block of 1024 rows (0 to 1023, 1024 to 2047, ..., all dimensions but the last counted through in order) at most 24 rows name the same one
- slot_map: int32 [128, 1024], P(('gx', 'gy')), may hold values from 0 to 511
- temp_solid: float32 [256, 256, 128], P('gx', 'gy'), may hold values from -6 to 6
- material: int32 [256, 256, 128], P('gx', 'gy'), may hold values from 0 to 3
Outputs:
- fluid_next: float32 [256, 512, 1024], P('gx', 'gy')
- wall_next: float32 [256, 512, 128], P('gx', 'gy')
- solid_next: float32 [256, 256, 128], P('gx', 'gy')
- stress_force: float32 [3, 256, 256, 128], P(None, 'gx', 'gy')
Inputs may be any that keep to these rules, and one draw needn't show every extreme that they name: `owner_map`: among the rows of one device, no owner is named by more than 24 rows, a bound that some block reaches.
All inputs are finite; a program needn't handle non-finite values. No bound on the sum of `wall_mask` on one device may be relied on, other than what follows from the above.
Results may differ from a plain program's by a relative error of at most 0.0003.
Values sent between devices are 32-bit elements; how exact they have to be, the bound alone decides.
A program may use at most 128 MiB of HBM per device.

v0:
```python
import jax
import jax.numpy as jnp
from jax import lax
from jax.sharding import PartitionSpec as P

FSTEPS = 2
SSTEPS = 4
NMAT = 4


time_step = 0.1
diffusivity = 0.5
film_coef = 2.0
solid_step = 0.05
source_gain = 4.0
conduct_table = (0.4, 0.9, 1.5, 2.2)
modulus_table = (0.5, 1.0, 1.6, 2.4)


def extended(value, sides, width):
    for axis, dim in sides:
        size, length = (lax.axis_size(axis), value.shape[dim])
        up = [(i, (i + 1) % size) for i in range(size - 1)]
        down = [(j, i) for i, j in up]
        last = lax.slice_in_dim(value, length - width, length, axis=dim)
        first = lax.slice_in_dim(value, 0, width, axis=dim)
        before = lax.ppermute(last, axis, up)
        after = lax.ppermute(first, axis, down)
        value = jnp.concatenate([before, value, after], axis=dim)
    return value


def laplace(padded):
    center = padded[1:-1, 1:-1, 1:-1]
    beside = padded[2:, 1:-1, 1:-1] + padded[:-2, 1:-1, 1:-1]
    beside = beside + padded[1:-1, 2:, 1:-1] + padded[1:-1, :-2, 1:-1]
    beside = beside + padded[1:-1, 1:-1, 2:] + padded[1:-1, 1:-1, :-2]
    return beside - 6.0 * center


def advect(padded, velocity):
    center = padded[1:-1, 1:-1, 1:-1]
    uppers = (padded[2:, 1:-1, 1:-1], padded[1:-1, 2:, 1:-1], padded[1:-1, 1:-1, 2:])
    lowers = (padded[:-2, 1:-1, 1:-1], padded[1:-1, :-2, 1:-1], padded[1:-1, 1:-1, :-2])
    total = jnp.zeros_like(center)
    for comp in range(3):
        speed = velocity[comp].astype(jnp.float32)
        total = (
            total
            + jnp.maximum(speed, 0.0) * (center - lowers[comp])
            + jnp.minimum(speed, 0.0) * (uppers[comp] - center)
        )
    return total


def fluid_update(padded, velocity, sink):
    center = padded[1:-1, 1:-1, 1:-1]
    return (
        center
        + time_step * (diffusivity * laplace(padded) - advect(padded, velocity))
        - time_step * sink
    )


def table_lookup(material, table):
    out = jnp.zeros(material.shape, jnp.float32)
    for index in range(NMAT):
        out = out + jnp.where(material == index, table[index], 0.0).astype(jnp.float32)
    return out


def solid_update(padded, cond, heat):
    center = padded[1:-1, 1:-1, 1:-1]
    return center + solid_step * (cond * laplace(padded) + source_gain * heat)


def gradient(padded):
    first = 0.5 * (padded[2:, 1:-1, 1:-1] - padded[:-2, 1:-1, 1:-1])
    second = 0.5 * (padded[1:-1, 2:, 1:-1] - padded[1:-1, :-2, 1:-1])
    third = 0.5 * (padded[1:-1, 1:-1, 2:] - padded[1:-1, 1:-1, :-2])
    return jnp.stack([first, second, third])


def pad_depth(padded):
    return jnp.pad(padded, ((0, 0), (0, 0), (1, 1)))


def fluid_faces(field):
    return pad_depth(extended(field, (("gx", 0), ("gy", 1)), 1))


def solid_faces(field):
    return pad_depth(extended(field, (("gx", 0), ("gy", 1)), 1))


def body(temp_fluid, velocity, wall_old, wall_mask, owner_map, slot_map, temp_solid, material):
    cells_x, cells_y, depth = temp_fluid.shape
    row_len = wall_old.shape[2]
    solid_x, solid_y, solid_z = temp_solid.shape
    count_x = lax.axis_size("gx")
    count_y = lax.axis_size("gy")
    ndevices = count_x * count_y
    row_count = cells_x * cells_y
    capacity = max(2, (3 * row_count + ndevices - 1) // ndevices)
    flux = wall_mask.astype(jnp.float32) * film_coef * (temp_fluid[:, :, :row_len] - wall_old)
    flux_rows = flux.reshape(row_count, row_len)
    owner = owner_map[0, :, 0]
    slot = slot_map[0]
    onehot = (owner[:, None] == jnp.arange(ndevices, dtype=jnp.int32)[None, :]).astype(jnp.int32)
    ranks = jnp.cumsum(onehot, axis=0) - 1
    position = jnp.sum(onehot * ranks, axis=1)
    outgoing = (
        jnp.zeros((ndevices, capacity, row_len), jnp.float32).at[owner, position].set(flux_rows)
    )
    out_slots = (
        jnp.zeros((ndevices, capacity), jnp.float32)
        .at[owner, position]
        .set(slot.astype(jnp.float32))
    )
    incoming, in_slots = (
        lax.all_to_all(outgoing, ("gx", "gy"), split_axis=0, concat_axis=0, tiled=True),
        lax.all_to_all(out_slots, ("gx", "gy"), split_axis=0, concat_axis=0, tiled=True),
    )
    sink = jnp.concatenate(
        [flux, jnp.zeros((cells_x, cells_y, depth - row_len), jnp.float32)], axis=2
    )
    slot_index = in_slots.astype(jnp.int32).reshape(-1)
    heat = (
        jnp.zeros((solid_x * solid_y, row_len), jnp.float32)
        .at[slot_index]
        .add(incoming.reshape(-1, row_len))
    )
    heat = heat.reshape(solid_x, solid_y, solid_z)
    cond = table_lookup(material, conduct_table)
    modulus = table_lookup(material, modulus_table)
    fluid = temp_fluid
    for step in range(FSTEPS):
        fluid = fluid_update(fluid_faces(fluid), velocity, sink)
    solid = temp_solid
    for step in range(SSTEPS):
        solid = solid_update(solid_faces(solid), cond, heat)
    stress_pad = pad_depth(extended(modulus * solid, (("gx", 0), ("gy", 1)), 1))
    stress_force = gradient(stress_pad)
    replies = solid.reshape(solid_x * solid_y, row_len)[slot_index].reshape(
        ndevices, capacity, row_len
    )
    returned = lax.all_to_all(replies, ("gx", "gy"), split_axis=0, concat_axis=0, tiled=True)
    wall_next = returned[owner, position].reshape(cells_x, cells_y, row_len)
    return (fluid, wall_next, solid, stress_force)


def solution(mesh):
    placed = (
        P("gx", "gy", None),
        P(None, "gx", "gy", None),
        P("gx", "gy", None),
        P("gx", "gy", None),
        P(("gx", "gy"), None, None),
        P(("gx", "gy"), None),
        P("gx", "gy", None),
        P("gx", "gy", None),
    )
    return jax.shard_map(
        body,
        mesh=mesh,
        in_specs=placed,
        out_specs=(
            P("gx", "gy", None),
            P("gx", "gy", None),
            P("gx", "gy", None),
            P(None, "gx", "gy", None),
        ),
        check_vma=False,
    )
```

profile of v0, /device:TPU:1, one launch (start us, length us, event | category | flops | bytes accessed | tf_op | source)
XLA Modules:
  0.0 253.6 jit_solution(3498642124309556237)
XLA Ops:
  0.7 2.0 fusion.111
  2.7 6.2 %collective-permute-start.1 = (f32[1,64,1024]{2,1,0:T(8,128)}, f32[1,64,1024]{2,1,0:T(8,128)S(1)}, u32[]{:S(2)}, u32[]{:S(2)}) collective-permute-start(f32[1,64,1024]{2,1,0:T(8,128)} %get-tuple-element.24), channel_id=1, source_target_pairs={{0,8},{8,16},{16,24},{24,32},{32,40},{40,48},{48,56},{56,64},{64,7... | collective-permute-start | bytes 786440 | tf_op jit(solution)/shard_map/ppermute | solution.py:27
  8.9 1.9 collective-permute-start
  10.8 0.8 copy.53
  11.6 0.2 fusion.61
  12.0 1.0 fusion.60
  13.4 4.3 %scatter_custom_fusion.1 = f32[3072]{0:T(1024)S(1)} fusion(s32[1024]{0:T(1024)S(1)} %get-tuple-element.51, f32[1024]{0:T(1024)S(1)} %bitcast.144, f32[]{:T(128)} %constant.22.clone.1), kind=kCustom, calls=%fused_computation.246 | custom fusion | bytes 12292
  17.7 0.7 copy.55
  18.4 10.4 %all-to-all-start = ((f32[128,1,24]{2,1,0:T(1,128)}), f32[128,1,24]{2,1,0:T(1,128)S(1)}, u32[]{:S(2)}, u32[]{:S(2)}) async-start(f32[128,1,24]{2,1,0:T(1,128)} %copy.55), calls=%async_computation | async-start | bytes 131072 | tf_op jit(solution)/shard_map/all_to_all | solution.py:122
  28.9 5.1 %collective-permute-start.9 = (f32[1,32,128]{2,1,0:T(8,128)S(1)}, f32[1,32,128]{2,1,0:T(8,128)S(1)}, u32[]{:S(2)}, u32[]{:S(2)}) collective-permute-start(f32[1,32,128]{2,1,0:T(8,128)S(1)} %get-tuple-element.46), channel_id=1, source_target_pairs={{0,8},{8,16},{16,24},{24,32},{32,40},{40,48},{48,56},{56,64},{64,7... | collective-permute-start | bytes 49160 | tf_op jit(solution)/shard_map/ppermute | solution.py:27
  33.9 1.9 collective-permute-start.8
  35.9 1.2 subtract_multiply_fusion
  37.1 4.3 %scatter_custom_fusion.2 = f32[3072,128]{1,0:T(8,128)} fusion(s32[1024]{0:T(1024)S(1)} %get-tuple-element.50, f32[1024,128]{1,0:T(8,128)S(1)} %bitcast.136, f32[]{:T(128)} %constant.22.clone.1), kind=kCustom, calls=%fused_computation.92 | custom fusion | bytes 1572868
  41.4 10.3 %all-to-all-start.1 = ((f32[128,24,128]{2,1,0:T(8,128)}), f32[128,24,128]{2,1,0:T(8,128)}, u32[]{:S(2)}, u32[]{:S(2)}) async-start(f32[128,24,128]{2,1,0:T(8,128)} %bitcast.19), calls=%async_computation.1 | async-start | bytes 3145728 | tf_op jit(solution)/shard_map/all_to_all | solution.py:121
  51.6 0.2 convert_reduce_fusion
  52.0 1.3 collective-permute-start.10
  53.3 4.0 %collective-permute-start.11 = (f32[18,1,128]{2,1,0:T(1,128)S(1)}, f32[18,1,128]{2,1,0:T(1,128)S(1)}, u32[]{:S(2)}, u32[]{:S(2)}) collective-permute-start(f32[18,1,128]{2,1,0:T(1,128)S(1)} %get-tuple-element.35), channel_id=1, source_target_pairs={{0,1},{1,2},{2,3},{3,4},{4,5},{5,6},{6,7},{8,9},{9,10},{10,11},{11... | collective-permute-start | bytes 27656 | tf_op jit(solution)/shard_map/ppermute | solution.py:27
  57.4 12.4 %collective-permute-done.10 = f32[18,1,128]{2,1,0:T(1,128)S(1)} collective-permute-done((f32[18,1,128]{2,1,0:T(1,128)S(1)}, f32[18,1,128]{2,1,0:T(1,128)S(1)}, u32[]{:S(2)}, u32[]{:S(2)}) %collective-permute-start.10) | collective-permute-done | bytes 9248 | tf_op jit(solution)/shard_map/ppermute | solution.py:28
  69.8 0.3 select_maximum_fusion.22
  70.1 2.5 %constant_dynamic-update-slice_fusion.1 = f32[18,64,1024]{2,1,0:T(8,128)S(1)} fusion(f32[18,64,1024]{2,1,0:T(8,128)S(1)} %constant_dynamic-update-slice_fusion.2, f32[16,64,1024]{2,1,0:T(8,128)} %param.8), kind=kLoop, calls=%fused_computation.225 | loop fusion | bytes 8388608
  72.7 2.1 copy-done.3
  75.0 1.3 collective-permute-start.2
  76.3 4.0 %collective-permute-start.3 = (f32[18,1,1024]{2,0,1:T(8,128)S(1)}, f32[18,1,1024]{2,0,1:T(8,128)S(1)}, u32[]{:S(2)}, u32[]{:S(2)}) collective-permute-start(f32[18,1,1024]{2,0,1:T(8,128)S(1)} %copy.43), channel_id=1, source_target_pairs={{0,1},{1,2},{2,3},{3,4},{4,5},{5,6},{6,7},{8,9},{9,10},{10,11},{11... | collective-permute-start | bytes 221192 | tf_op jit(solution)/shard_map/ppermute | solution.py:27
  80.3 17.6 %scatter_custom_fusion = f32[512,128]{1,0:T(8,128)S(1)} fusion(s32[3072]{0:T(1024)S(1)} %bitcast.139, f32[3072,128]{1,0:T(8,128)} %bitcast.20, f32[]{:T(128)} %constant.22.clone.1), kind=kCustom, calls=%fused_computation.210 | custom fusion | flops 393216 | bytes 262656 | tf_op jit(solution)/shard_map/scatter-add | solution.py:131
  98.0 0.4 fusion.99
  98.5 3.3 %collective-permute-start.12 = (f32[1,32,128]{2,1,0:T(8,128)S(1)}, f32[1,32,128]{2,1,0:T(8,128)S(1)}, u32[]{:S(2)}, u32[]{:S(2)}) collective-permute-start(f32[1,32,128]{2,1,0:T(8,128)S(1)} %get-tuple-element.44), channel_id=1, source_target_pairs={{8,0},{16,8},{24,16},{32,24},{40,32},{48,40},{56,48},{64,56},{72,6... | collective-permute-start | bytes 49160 | tf_op jit(solution)/shard_map/ppermute | solution.py:28
  101.7 4.5 %collective-permute-start.13 = (f32[1,32,128]{2,1,0:T(8,128)S(1)}, f32[1,32,128]{2,1,0:T(8,128)S(1)}, u32[]{:S(2)}, u32[]{:S(2)}) collective-permute-start(f32[1,32,128]{2,1,0:T(8,128)S(1)} %get-tuple-element.43), channel_id=1, source_target_pairs={{0,8},{8,16},{16,24},{24,32},{32,40},{40,48},{48,56},{56,64},{64,7... | collective-permute-start | bytes 49160 | tf_op jit(solution)/shard_map/ppermute | solution.py:27
  106.5 0.6 collective-permute-done.13
  107.1 1.3 collective-permute-start.14
  108.5 4.2 %collective-permute-start.15 = (f32[18,1,128]{2,1,0:T(1,128)S(1)}, f32[18,1,128]{2,1,0:T(1,128)S(1)}, u32[]{:S(2)}, u32[]{:S(2)}) collective-permute-start(f32[18,1,128]{2,1,0:T(1,128)S(1)} %get-tuple-element.33), channel_id=1, source_target_pairs={{0,1},{1,2},{2,3},{3,4},{4,5},{5,6},{6,7},{8,9},{9,10},{10,11},{11... | collective-permute-start | bytes 27656 | tf_op jit(solution)/shard_map/ppermute | solution.py:27
  112.7 4.7 %select_maximum_fusion.4 = f32[18,66,1026]{2,1,0:T(8,128)S(1)} fusion(f32[18,1,1024]{2,1,0:T(1,128)S(1)} %copy.42, f32[18,64,1024]{2,1,0:T(8,128)} %copy-done.3, f32[18,1,1024]{2,1,0:T(1,128)S(1)} %copy.44), kind=kLoop, calls=%fused_computation.11 | loop fusion | flops 9751104 | bytes 9741600 | tf_op jit(solution)/shard_map/concatenate | solution.py:29
  117.4 0.3 select_maximum_fusion.18
  117.8 0.3 fusion.91
  118.1 2.1 collective-permute-start.16
  120.2 6.3 %collective-permute-start.17 = (f32[1,32,128]{2,1,0:T(8,128)S(1)}, f32[1,32,128]{2,1,0:T(8,128)S(1)}, u32[]{:S(2)}, u32[]{:S(2)}) collective-permute-start(f32[1,32,128]{2,1,0:T(8,128)S(1)} %get-tuple-element.41), channel_id=1, source_target_pairs={{0,8},{8,16},{16,24},{24,32},{32,40},{40,48},{48,56},{56,64},{64,7... | collective-permute-start | bytes 49160 | tf_op jit(solution)/shard_map/ppermute | solution.py:27
  126.6 9.4 %fusion.12 = f32[16,64,1024]{2,1,0:T(8,128)S(1)} fusion(f32[16,64,1024]{2,1,0:T(8,128)S(1)} %copy-done.2, f32[1,64,1024]{2,1,0:T(8,128)S(1)} %collective-permute-done.1, f32[1,64,1024]{2,1,0:T(8,128)S(1)} %collective-permute-done, f32[16,64,128]{2,1,0:T(8,128)S(1)} %subtract_multiply_fusion, f32[18,66,1026]{2,1,0:T(8,128)S(1)} %select_maximum_fusion.4, ...), kind=kLoop, calls=%fused_computation.31 | loop fusion | flops 45088768 | bytes 28983296 | tf_op jit(solution)/shard_map/sub | solution.py:59
  136.1 1.3 collective-permute-start.18
  137.4 5.2 %collective-permute-start.19 = (f32[18,1,128]{2,1,0:T(1,128)S(1)}, f32[18,1,128]{2,1,0:T(1,128)S(1)}, u32[]{:S(2)}, u32[]{:S(2)}) collective-permute-start(f32[18,1,128]{2,1,0:T(1,128)S(1)} %get-tuple-element.31), channel_id=1, source_target_pairs={{0,1},{1,2},{2,3},{3,4},{4,5},{5,6},{6,7},{8,9},{9,10},{10,11},{11... | collective-permute-start | bytes 27656 | tf_op jit(solution)/shard_map/ppermute | solution.py:27
  142.6 1.9 collective-permute-start.4
  144.5 5.1 %collective-permute-start.5 = (f32[1,64,1024]{2,1,0:T(8,128)S(1)}, f32[1,64,1024]{2,1,0:T(8,128)S(1)}, u32[]{:S(2)}, u32[]{:S(2)}) collective-permute-start(f32[1,64,1024]{2,1,0:T(8,128)S(1)} %get-tuple-element.21), channel_id=1, source_target_pairs={{0,8},{8,16},{16,24},{24,32},{32,40},{40,48},{48,56},{56,64},{64,7... | collective-permute-start | bytes 786440 | tf_op jit(solution)/shard_map/ppermute | solution.py:27
  149.7 0.3 select_maximum_fusion.14
  150.1 0.3 fusion.83
  150.4 1.9 collective-permute-start.20
  152.4 5.1 %collective-permute-start.21 = (f32[1,32,128]{2,1,0:T(8,128)S(1)}, f32[1,32,128]{2,1,0:T(8,128)S(1)}, u32[]{:S(2)}, u32[]{:S(2)}) collective-permute-start(f32[1,32,128]{2,1,0:T(8,128)S(1)} %get-tuple-element.39), channel_id=1, source_target_pairs={{0,8},{8,16},{16,24},{24,32},{32,40},{40,48},{48,56},{56,64},{64,7... | collective-permute-start | bytes 49160 | tf_op jit(solution)/shard_map/ppermute | solution.py:27
  157.5 0.1 pad_maximum_fusion.51
  157.7 3.8 %collective-permute-start.7 = (f32[18,1,1024]{2,0,1:T(8,128)S(1)}, f32[18,1,1024]{2,0,1:T(8,128)S(1)}, u32[]{:S(2)}, u32[]{:S(2)}) collective-permute-start(f32[18,1,1024]{2,0,1:T(8,128)S(1)} %copy.49), channel_id=1, source_target_pairs={{0,1},{1,2},{2,3},{3,4},{4,5},{5,6},{6,7},{8,9},{9,10},{10,11},{11... | collective-permute-start | bytes 221192 | tf_op jit(solution)/shard_map/ppermute | solution.py:27
  161.5 1.3 collective-permute-start.6
  162.9 1.3 collective-permute-start.22
  164.2 7.0 %collective-permute-start.23 = (f32[18,1,128]{2,1,0:T(1,128)S(1)}, f32[18,1,128]{2,1,0:T(1,128)S(1)}, u32[]{:S(2)}, u32[]{:S(2)}) collective-permute-start(f32[18,1,128]{2,1,0:T(1,128)S(1)} %get-tuple-element.29), channel_id=1, source_target_pairs={{0,1},{1,2},{2,3},{3,4},{4,5},{5,6},{6,7},{8,9},{9,10},{10,11},{11... | collective-permute-start | bytes 27656 | tf_op jit(solution)/shard_map/ppermute | solution.py:27
  171.4 0.6 collective-permute-done.23
  172.0 0.3 select_maximum_fusion.10
  172.3 0.4 add_multiply_fusion
  172.7 1.9 collective-permute-start.24
  174.7 5.1 %collective-permute-start.25 = (f32[1,32,128]{2,1,0:T(8,128)S(1)}, f32[1,32,128]{2,1,0:T(8,128)S(1)}, u32[]{:S(2)}, u32[]{:S(2)}) collective-permute-start(f32[1,32,128]{2,1,0:T(8,128)S(1)} %get-tuple-element.37), channel_id=1, source_target_pairs={{0,8},{8,16},{16,24},{24,32},{32,40},{40,48},{48,56},{56,64},{64,7... | collective-permute-start | bytes 49160 | tf_op jit(solution)/shard_map/ppermute | solution.py:27
  179.8 7.2 %select_maximum_fusion = f32[18,66,1026]{2,1,0:T(8,128)} fusion(f32[18,1,1024]{2,1,0:T(1,128)S(1)} %copy.48, f32[18,1,1024]{2,1,0:T(1,128)S(1)} %copy.50, f32[1,64,1024]{2,1,0:T(8,128)S(1)} %collective-permute-done.4, f32[16,64,1024]{2,1,0:T(8,128)S(1)} %fusion.12, f32[1,64,1024]{2,1,0:T(8,128)S(1)} %collective-permute-done.5), kind=kLoop, calls=%fused_computation.7 | loop fusion | flops 14626656 | bytes 9741600 | tf_op jit(solution)/shard_map/concatenate | solution.py:29
  187.0 10.8 %gather_fusion = f32[3072,128]{1,0:T(8,128)} fusion(f32[512,128]{1,0:T(8,128)S(1)} %bitcast.128, s32[3072]{0:T(1024)S(1)} %broadcast_clamp_fusion), kind=kCustom, calls=%fused_computation | custom fusion | bytes 3158016 | tf_op jit(solution)/shard_map/gather | solution.py:144
  197.8 17.6 %all-to-all-start.2 = ((f32[128,24,128]{2,1,0:T(8,128)}), f32[128,24,128]{2,1,0:T(8,128)S(1)}, u32[]{:S(2)}, u32[]{:S(2)}) async-start(f32[128,24,128]{2,1,0:T(8,128)} %bitcast.23), calls=%async_computation.2 | async-start | bytes 3145728 | tf_op jit(solution)/shard_map/all_to_all | solution.py:147
  215.5 1.3 collective-permute-start.26
  216.8 4.2 %collective-permute-start.27 = (f32[18,1,128]{2,1,0:T(1,128)S(1)}, f32[18,1,128]{2,1,0:T(1,128)S(1)}, u32[]{:S(2)}, u32[]{:S(2)}) collective-permute-start(f32[18,1,128]{2,1,0:T(1,128)S(1)} %get-tuple-element.27), channel_id=1, source_target_pairs={{0,1},{1,2},{2,3},{3,4},{4,5},{5,6},{6,7},{8,9},{9,10},{10,11},{11... | collective-permute-start | bytes 27656 | tf_op jit(solution)/shard_map/ppermute | solution.py:27
  221.0 19.5 %fusion.21 = f32[16,64,1024]{2,1,0:T(8,128)} fusion(f32[16,64,1024]{2,1,0:T(8,128)} %copy-done.1, f32[1,64,1024]{2,1,0:T(8,128)S(1)} %collective-permute-done.4, f32[1,64,1024]{2,1,0:T(8,128)S(1)} %collective-permute-done.5, f32[18,1,1024]{2,1,0:T(1,128)S(1)} %copy.50, f32[18,1,1024]{2,1,0:T(1,128)S(1)} %copy.48, f32[18,66,1026]{2,1,0:T(8,128)} %select_maximum_fusion, ...), kind=kLoop, calls=%fused_computation.40 | loop fusion | flops 49283072 | bytes 24264704 | tf_op jit(solution)/shard_map/sub | solution.py:59
  240.6 0.3 select_maximum_fusion.6
  240.9 0.1 fusion.64
  241.1 0.9 pad_maximum_fusion.12
  242.0 11.6 %gather_fusion.1 = f32[1024,128]{1,0:T(8,128)} fusion(f32[128,24,128]{2,1,0:T(8,128)S(1)} %all-to-all-done.2, s32[1024]{0:T(1024)S(1)} %bitcast.129), kind=kCustom, calls=%fused_computation.1 | custom fusion | bytes 1056768 | tf_op jit(solution)/shard_map/gather | solution.py:148
  (100 shorter events, 1.5 us)
Async XLA Ops:
  0.6 12.5 %copy-start.13 = (s32[2]{0:T(128)S(1)}, s32[2]{0:T(128)}, u32[]{:S(2)}) copy-start(s32[2]{0:T(128)} %constant.82) | copy-start | bytes 28
  0.6 12.6 %copy-start.11 = (s32[2]{0:T(128)S(1)}, s32[2]{0:T(128)}, u32[]{:S(2)}) copy-start(s32[2]{0:T(128)} %constant.85) | copy-start | bytes 28
  0.7 12.6 %copy-start.12 = (s32[2]{0:T(128)S(1)}, s32[2]{0:T(128)}, u32[]{:S(2)}) copy-start(s32[2]{0:T(128)} %constant.79) | copy-start | bytes 28
  0.7 12.4 %copy-start.9 = (s32[1,1024,1]{1,2,0:T(1,128)S(1)}, s32[1,1024,1]{1,2,0:T(1,128)}, u32[]{:S(2)}) copy-start(s32[1,1024,1]{1,2,0:T(1,128)} %param.12) | copy-start | bytes 12292
  0.7 12.4 %copy-start.10 = (s32[1,1024]{1,0:T(1,128)S(1)}, s32[1,1024]{1,0:T(1,128)}, u32[]{:S(2)}) copy-start(s32[1,1024]{1,0:T(1,128)} %param.13) | copy-start | bytes 12292
  0.7 28.2 %copy-start.5 = (f32[16,32,128]{2,1,0:T(8,128)S(1)}, f32[16,32,128]{2,1,0:T(8,128)}, u32[]{:S(2)}) copy-start(f32[16,32,128]{2,1,0:T(8,128)} %param.14) | copy-start | bytes 786436
  0.7 35.2 %copy-start.6 = (f32[16,64,128]{2,1,0:T(8,128)S(1)}, f32[16,64,128]{2,1,0:T(8,128)}, u32[]{:S(2)}) copy-start(f32[16,64,128]{2,1,0:T(8,128)} %param.10) | copy-start | bytes 1572868
  0.7 35.2 %copy-start.7 = (s32[16,64,128]{2,1,0:T(8,128)S(1)}, s32[16,64,128]{2,1,0:T(8,128)}, u32[]{:S(2)}) copy-start(s32[16,64,128]{2,1,0:T(8,128)} %param.11) | copy-start | bytes 1572868
  2.7 67.4 %collective-permute-start.1 = (f32[1,64,1024]{2,1,0:T(8,128)}, f32[1,64,1024]{2,1,0:T(8,128)S(1)}, u32[]{:S(2)}, u32[]{:S(2)}) collective-permute-start(f32[1,64,1024]{2,1,0:T(8,128)} %get-tuple-element.24), channel_id=1, source_target_pairs={{0,8},{8,16},{16,24},{24,32},{32,40},{40,48},{48,56},{56,64},{64,7... | collective-permute-start | bytes 786440 | tf_op jit(solution)/shard_map/ppermute | solution.py:27
  8.9 63.8 %collective-permute-start = (f32[1,64,1024]{2,1,0:T(8,128)}, f32[1,64,1024]{2,1,0:T(8,128)S(1)}, u32[]{:S(2)}, u32[]{:S(2)}) collective-permute-start(f32[1,64,1024]{2,1,0:T(8,128)} %get-tuple-element.23), channel_id=1, source_target_pairs={{8,0},{16,8},{24,16},{32,24},{40,32},{48,40},{56,48},{64,56},{72,6... | collective-permute-start | bytes 786440 | tf_op jit(solution)/shard_map/ppermute | solution.py:28
  18.4 22.9 %all-to-all-start = ((f32[128,1,24]{2,1,0:T(1,128)}), f32[128,1,24]{2,1,0:T(1,128)S(1)}, u32[]{:S(2)}, u32[]{:S(2)}) async-start(f32[128,1,24]{2,1,0:T(1,128)} %copy.55), calls=%async_computation | async-start | bytes 131072 | tf_op jit(solution)/shard_map/all_to_all | solution.py:122
  28.9 23.1 %collective-permute-start.9 = (f32[1,32,128]{2,1,0:T(8,128)S(1)}, f32[1,32,128]{2,1,0:T(8,128)S(1)}, u32[]{:S(2)}, u32[]{:S(2)}) collective-permute-start(f32[1,32,128]{2,1,0:T(8,128)S(1)} %get-tuple-element.46), channel_id=1, source_target_pairs={{0,8},{8,16},{16,24},{24,32},{32,40},{40,48},{48,56},{56,64},{64,7... | collective-permute-start | bytes 49160 | tf_op jit(solution)/shard_map/ppermute | solution.py:27
  33.9 18.1 %collective-permute-start.8 = (f32[1,32,128]{2,1,0:T(8,128)S(1)}, f32[1,32,128]{2,1,0:T(8,128)S(1)}, u32[]{:S(2)}, u32[]{:S(2)}) collective-permute-start(f32[1,32,128]{2,1,0:T(8,128)S(1)} %get-tuple-element.45), channel_id=1, source_target_pairs={{8,0},{16,8},{24,16},{32,24},{40,32},{48,40},{56,48},{64,56},{72,6... | collective-permute-start | bytes 49160 | tf_op jit(solution)/shard_map/ppermute | solution.py:28
  41.4 39.0 %all-to-all-start.1 = ((f32[128,24,128]{2,1,0:T(8,128)}), f32[128,24,128]{2,1,0:T(8,128)}, u32[]{:S(2)}, u32[]{:S(2)}) async-start(f32[128,24,128]{2,1,0:T(8,128)} %bitcast.19), calls=%async_computation.1 | async-start | bytes 3145728 | tf_op jit(solution)/shard_map/all_to_all | solution.py:121
  52.0 17.7 %collective-permute-start.10 = (f32[18,1,128]{2,1,0:T(1,128)S(1)}, f32[18,1,128]{2,1,0:T(1,128)S(1)}, u32[]{:S(2)}, u32[]{:S(2)}) collective-permute-start(f32[18,1,128]{2,1,0:T(1,128)S(1)} %get-tuple-element.36), channel_id=1, source_target_pairs={{1,0},{2,1},{3,2},{4,3},{5,4},{6,5},{7,6},{9,8},{10,9},{11,10},{12... | collective-permute-start | bytes 27656 | tf_op jit(solution)/shard_map/ppermute | solution.py:28
  53.3 16.4 %collective-permute-start.11 = (f32[18,1,128]{2,1,0:T(1,128)S(1)}, f32[18,1,128]{2,1,0:T(1,128)S(1)}, u32[]{:S(2)}, u32[]{:S(2)}) collective-permute-start(f32[18,1,128]{2,1,0:T(1,128)S(1)} %get-tuple-element.35), channel_id=1, source_target_pairs={{0,1},{1,2},{2,3},{3,4},{4,5},{5,6},{6,7},{8,9},{9,10},{10,11},{11... | collective-permute-start | bytes 27656 | tf_op jit(solution)/shard_map/ppermute | solution.py:27
  70.1 27.9 %copy-start.8 = (s32[16,32,128]{2,1,0:T(8,128)S(1)}, s32[16,32,128]{2,1,0:T(8,128)}, u32[]{:S(2)}) copy-start(s32[16,32,128]{2,1,0:T(8,128)} %param.15) | copy-start | bytes 786436
  72.7 2.1 copy-start.3
  75.0 31.2 %collective-permute-start.2 = (f32[18,1,1024]{2,0,1:T(8,128)S(1)}, f32[18,1,1024]{2,0,1:T(8,128)S(1)}, u32[]{:S(2)}, u32[]{:S(2)}) collective-permute-start(f32[18,1,1024]{2,0,1:T(8,128)S(1)} %copy.41), channel_id=1, source_target_pairs={{1,0},{2,1},{3,2},{4,3},{5,4},{6,5},{7,6},{9,8},{10,9},{11,10},{12... | collective-permute-start | bytes 221192 | tf_op jit(solution)/shard_map/ppermute | solution.py:28
  76.3 30.0 %collective-permute-start.3 = (f32[18,1,1024]{2,0,1:T(8,128)S(1)}, f32[18,1,1024]{2,0,1:T(8,128)S(1)}, u32[]{:S(2)}, u32[]{:S(2)}) collective-permute-start(f32[18,1,1024]{2,0,1:T(8,128)S(1)} %copy.43), channel_id=1, source_target_pairs={{0,1},{1,2},{2,3},{3,4},{4,5},{5,6},{6,7},{8,9},{9,10},{10,11},{11... | collective-permute-start | bytes 221192 | tf_op jit(solution)/shard_map/ppermute | solution.py:27
  98.0 28.5 %copy-start.4 = (f32[18,64,1024]{2,1,0:T(8,128)S(1)}, f32[18,64,1024]{2,1,0:T(8,128)}, u32[]{:S(2)}) copy-start(f32[18,64,1024]{2,1,0:T(8,128)} %copy-done.3) | copy-start | bytes 14155780
  98.5 8.0 %collective-permute-start.12 = (f32[1,32,128]{2,1,0:T(8,128)S(1)}, f32[1,32,128]{2,1,0:T(8,128)S(1)}, u32[]{:S(2)}, u32[]{:S(2)}) collective-permute-start(f32[1,32,128]{2,1,0:T(8,128)S(1)} %get-tuple-element.44), channel_id=1, source_target_pairs={{8,0},{16,8},{24,16},{32,24},{40,32},{48,40},{56,48},{64,56},{72,6... | collective-permute-start | bytes 49160 | tf_op jit(solution)/shard_map/ppermute | solution.py:28
  101.7 5.4 %collective-permute-start.13 = (f32[1,32,128]{2,1,0:T(8,128)S(1)}, f32[1,32,128]{2,1,0:T(8,128)S(1)}, u32[]{:S(2)}, u32[]{:S(2)}) collective-permute-start(f32[1,32,128]{2,1,0:T(8,128)S(1)} %get-tuple-element.43), channel_id=1, source_target_pairs={{0,8},{8,16},{16,24},{24,32},{32,40},{40,48},{48,56},{56,64},{64,7... | collective-permute-start | bytes 49160 | tf_op jit(solution)/shard_map/ppermute | solution.py:27
  107.1 10.3 %collective-permute-start.14 = (f32[18,1,128]{2,1,0:T(1,128)S(1)}, f32[18,1,128]{2,1,0:T(1,128)S(1)}, u32[]{:S(2)}, u32[]{:S(2)}) collective-permute-start(f32[18,1,128]{2,1,0:T(1,128)S(1)} %get-tuple-element.34), channel_id=1, source_target_pairs={{1,0},{2,1},{3,2},{4,3},{5,4},{6,5},{7,6},{9,8},{10,9},{11,10},{12... | collective-permute-start | bytes 27656 | tf_op jit(solution)/shard_map/ppermute | solution.py:28
  108.4 18.1 %slice-start = ((s8[6291456]{0:T(1024)(128)(4,1)}), s8[4194304]{0:T(1024)(128)(4,1)S(1)}, s32[]{:S(2)}) async-start(s8[6291456]{0:T(1024)(128)(4,1)} %bitcast.130), calls=%async_computation.3 | async-start | bytes 8388608
  108.4 18.1 %slice-start.1 = ((s8[6291456]{0:T(1024)(128)(4,1)}), s8[2097152]{0:T(1024)(128)(4,1)S(1)}, s32[]{:S(2)}) async-start(s8[6291456]{0:T(1024)(128)(4,1)} %bitcast.130), calls=%async_computation.4 | async-start | bytes 4194304
  108.4 18.1 %copy-start.2 = (f32[16,64,1024]{2,1,0:T(8,128)S(1)}, f32[16,64,1024]{2,1,0:T(8,128)}, u32[]{:S(2)}) copy-start(f32[16,64,1024]{2,1,0:T(8,128)} %param.8) | copy-start | bytes 12582916
  108.5 9.0 %collective-permute-start.15 = (f32[18,1,128]{2,1,0:T(1,128)S(1)}, f32[18,1,128]{2,1,0:T(1,128)S(1)}, u32[]{:S(2)}, u32[]{:S(2)}) collective-permute-start(f32[18,1,128]{2,1,0:T(1,128)S(1)} %get-tuple-element.33), channel_id=1, source_target_pairs={{0,1},{1,2},{2,3},{3,4},{4,5},{5,6},{6,7},{8,9},{9,10},{10,11},{11... | collective-permute-start | bytes 27656 | tf_op jit(solution)/shard_map/ppermute | solution.py:27
  118.1 17.9 %collective-permute-start.16 = (f32[1,32,128]{2,1,0:T(8,128)S(1)}, f32[1,32,128]{2,1,0:T(8,128)S(1)}, u32[]{:S(2)}, u32[]{:S(2)}) collective-permute-start(f32[1,32,128]{2,1,0:T(8,128)S(1)} %get-tuple-element.42), channel_id=1, source_target_pairs={{8,0},{16,8},{24,16},{32,24},{40,32},{48,40},{56,48},{64,56},{72,6... | collective-permute-start | bytes 49160 | tf_op jit(solution)/shard_map/ppermute | solution.py:28
  120.2 15.8 %collective-permute-start.17 = (f32[1,32,128]{2,1,0:T(8,128)S(1)}, f32[1,32,128]{2,1,0:T(8,128)S(1)}, u32[]{:S(2)}, u32[]{:S(2)}) collective-permute-start(f32[1,32,128]{2,1,0:T(8,128)S(1)} %get-tuple-element.41), channel_id=1, source_target_pairs={{0,8},{8,16},{16,24},{24,32},{32,40},{40,48},{48,56},{56,64},{64,7... | collective-permute-start | bytes 49160 | tf_op jit(solution)/shard_map/ppermute | solution.py:27
  136.0 43.8 %copy-start.1 = (f32[16,64,1024]{2,1,0:T(8,128)}, f32[16,64,1024]{2,1,0:T(8,128)S(1)}, u32[]{:S(2)}) copy-start(f32[16,64,1024]{2,1,0:T(8,128)S(1)} %fusion.12) | copy-start | bytes 12582916
  136.1 13.6 %collective-permute-start.18 = (f32[18,1,128]{2,1,0:T(1,128)S(1)}, f32[18,1,128]{2,1,0:T(1,128)S(1)}, u32[]{:S(2)}, u32[]{:S(2)}) collective-permute-start(f32[18,1,128]{2,1,0:T(1,128)S(1)} %get-tuple-element.32), channel_id=1, source_target_pairs={{1,0},{2,1},{3,2},{4,3},{5,4},{6,5},{7,6},{9,8},{10,9},{11,10},{12... | collective-permute-start | bytes 27656 | tf_op jit(solution)/shard_map/ppermute | solution.py:28
  137.4 12.3 %collective-permute-start.19 = (f32[18,1,128]{2,1,0:T(1,128)S(1)}, f32[18,1,128]{2,1,0:T(1,128)S(1)}, u32[]{:S(2)}, u32[]{:S(2)}) collective-permute-start(f32[18,1,128]{2,1,0:T(1,128)S(1)} %get-tuple-element.31), channel_id=1, source_target_pairs={{0,1},{1,2},{2,3},{3,4},{4,5},{5,6},{6,7},{8,9},{9,10},{10,11},{11... | collective-permute-start | bytes 27656 | tf_op jit(solution)/shard_map/ppermute | solution.py:27
  142.6 14.9 %collective-permute-start.4 = (f32[1,64,1024]{2,1,0:T(8,128)S(1)}, f32[1,64,1024]{2,1,0:T(8,128)S(1)}, u32[]{:S(2)}, u32[]{:S(2)}) collective-permute-start(f32[1,64,1024]{2,1,0:T(8,128)S(1)} %get-tuple-element.22), channel_id=1, source_target_pairs={{8,0},{16,8},{24,16},{32,24},{40,32},{48,40},{56,48},{64,56},{72,6... | collective-permute-start | bytes 786440 | tf_op jit(solution)/shard_map/ppermute | solution.py:28
  144.5 13.0 %collective-permute-start.5 = (f32[1,64,1024]{2,1,0:T(8,128)S(1)}, f32[1,64,1024]{2,1,0:T(8,128)S(1)}, u32[]{:S(2)}, u32[]{:S(2)}) collective-permute-start(f32[1,64,1024]{2,1,0:T(8,128)S(1)} %get-tuple-element.21), channel_id=1, source_target_pairs={{0,8},{8,16},{16,24},{24,32},{32,40},{40,48},{48,56},{56,64},{64,7... | collective-permute-start | bytes 786440 | tf_op jit(solution)/shard_map/ppermute | solution.py:27
  150.4 12.4 %collective-permute-start.20 = (f32[1,32,128]{2,1,0:T(8,128)S(1)}, f32[1,32,128]{2,1,0:T(8,128)S(1)}, u32[]{:S(2)}, u32[]{:S(2)}) collective-permute-start(f32[1,32,128]{2,1,0:T(8,128)S(1)} %get-tuple-element.40), channel_id=1, source_target_pairs={{8,0},{16,8},{24,16},{32,24},{40,32},{48,40},{56,48},{64,56},{72,6... | collective-permute-start | bytes 49160 | tf_op jit(solution)/shard_map/ppermute | solution.py:28
  152.4 10.5 %collective-permute-start.21 = (f32[1,32,128]{2,1,0:T(8,128)S(1)}, f32[1,32,128]{2,1,0:T(8,128)S(1)}, u32[]{:S(2)}, u32[]{:S(2)}) collective-permute-start(f32[1,32,128]{2,1,0:T(8,128)S(1)} %get-tuple-element.39), channel_id=1, source_target_pairs={{0,8},{8,16},{16,24},{24,32},{32,40},{40,48},{48,56},{56,64},{64,7... | collective-permute-start | bytes 49160 | tf_op jit(solution)/shard_map/ppermute | solution.py:27
  157.7 13.5 %collective-permute-start.7 = (f32[18,1,1024]{2,0,1:T(8,128)S(1)}, f32[18,1,1024]{2,0,1:T(8,128)S(1)}, u32[]{:S(2)}, u32[]{:S(2)}) collective-permute-start(f32[18,1,1024]{2,0,1:T(8,128)S(1)} %copy.49), channel_id=1, source_target_pairs={{0,1},{1,2},{2,3},{3,4},{4,5},{5,6},{6,7},{8,9},{9,10},{10,11},{11... | collective-permute-start | bytes 221192 | tf_op jit(solution)/shard_map/ppermute | solution.py:27
  161.5 9.8 %collective-permute-start.6 = (f32[18,1,1024]{2,0,1:T(8,128)S(1)}, f32[18,1,1024]{2,0,1:T(8,128)S(1)}, u32[]{:S(2)}, u32[]{:S(2)}) collective-permute-start(f32[18,1,1024]{2,0,1:T(8,128)S(1)} %copy.47), channel_id=1, source_target_pairs={{1,0},{2,1},{3,2},{4,3},{5,4},{6,5},{7,6},{9,8},{10,9},{11,10},{12... | collective-permute-start | bytes 221192 | tf_op jit(solution)/shard_map/ppermute | solution.py:28
  162.9 8.5 %collective-permute-start.22 = (f32[18,1,128]{2,1,0:T(1,128)S(1)}, f32[18,1,128]{2,1,0:T(1,128)S(1)}, u32[]{:S(2)}, u32[]{:S(2)}) collective-permute-start(f32[18,1,128]{2,1,0:T(1,128)S(1)} %get-tuple-element.30), channel_id=1, source_target_pairs={{1,0},{2,1},{3,2},{4,3},{5,4},{6,5},{7,6},{9,8},{10,9},{11,10},{12... | collective-permute-start | bytes 27656 | tf_op jit(solution)/shard_map/ppermute | solution.py:28
  164.2 7.8 %collective-permute-start.23 = (f32[18,1,128]{2,1,0:T(1,128)S(1)}, f32[18,1,128]{2,1,0:T(1,128)S(1)}, u32[]{:S(2)}, u32[]{:S(2)}) collective-permute-start(f32[18,1,128]{2,1,0:T(1,128)S(1)} %get-tuple-element.29), channel_id=1, source_target_pairs={{0,1},{1,2},{2,3},{3,4},{4,5},{5,6},{6,7},{8,9},{9,10},{10,11},{11... | collective-permute-start | bytes 27656 | tf_op jit(solution)/shard_map/ppermute | solution.py:27
  172.7 14.3 %copy-start = (f32[16,32,128]{2,1,0:T(8,128)}, f32[16,32,128]{2,1,0:T(8,128)S(1)}, u32[]{:S(2)}) copy-start(f32[16,32,128]{2,1,0:T(8,128)S(1)} %get-tuple-element.11) | copy-start | bytes 786436
  172.7 42.7 %collective-permute-start.24 = (f32[1,32,128]{2,1,0:T(8,128)S(1)}, f32[1,32,128]{2,1,0:T(8,128)S(1)}, u32[]{:S(2)}, u32[]{:S(2)}) collective-permute-start(f32[1,32,128]{2,1,0:T(8,128)S(1)} %get-tuple-element.38), channel_id=1, source_target_pairs={{8,0},{16,8},{24,16},{32,24},{40,32},{48,40},{56,48},{64,56},{72,6... | collective-permute-start | bytes 49160 | tf_op jit(solution)/shard_map/ppermute | solution.py:28
  174.7 40.8 %collective-permute-start.25 = (f32[1,32,128]{2,1,0:T(8,128)S(1)}, f32[1,32,128]{2,1,0:T(8,128)S(1)}, u32[]{:S(2)}, u32[]{:S(2)}) collective-permute-start(f32[1,32,128]{2,1,0:T(8,128)S(1)} %get-tuple-element.37), channel_id=1, source_target_pairs={{0,8},{8,16},{16,24},{24,32},{32,40},{40,48},{48,56},{56,64},{64,7... | collective-permute-start | bytes 49160 | tf_op jit(solution)/shard_map/ppermute | solution.py:27
  197.8 44.2 %all-to-all-start.2 = ((f32[128,24,128]{2,1,0:T(8,128)}), f32[128,24,128]{2,1,0:T(8,128)S(1)}, u32[]{:S(2)}, u32[]{:S(2)}) async-start(f32[128,24,128]{2,1,0:T(8,128)} %bitcast.23), calls=%async_computation.2 | async-start | bytes 3145728 | tf_op jit(solution)/shard_map/all_to_all | solution.py:147
  215.5 25.0 %collective-permute-start.26 = (f32[18,1,128]{2,1,0:T(1,128)S(1)}, f32[18,1,128]{2,1,0:T(1,128)S(1)}, u32[]{:S(2)}, u32[]{:S(2)}) collective-permute-start(f32[18,1,128]{2,1,0:T(1,128)S(1)} %get-tuple-element.28), channel_id=1, source_target_pairs={{1,0},{2,1},{3,2},{4,3},{5,4},{6,5},{7,6},{9,8},{10,9},{11,10},{12... | collective-permute-start | bytes 27656 | tf_op jit(solution)/shard_map/ppermute | solution.py:28
  216.8 23.7 %collective-permute-start.27 = (f32[18,1,128]{2,1,0:T(1,128)S(1)}, f32[18,1,128]{2,1,0:T(1,128)S(1)}, u32[]{:S(2)}, u32[]{:S(2)}) collective-permute-start(f32[18,1,128]{2,1,0:T(1,128)S(1)} %get-tuple-element.27), channel_id=1, source_target_pairs={{0,1},{1,2},{2,3},{3,4},{4,5},{5,6},{6,7},{8,9},{9,10},{10,11},{11... | collective-permute-start | bytes 27656 | tf_op jit(solution)/shard_map/ppermute | solution.py:27
where the time goes:
time: 256 us; the launch traced here: 254 us
  starting transfers between devices  132 us (52%)
  other arithmetic  66 us (26%)
  local copies, waits for them, and re-layouts  40.1 us (16%)
  waiting for transfers between devices  13.7 us (5%)
    ppermute x14, starting transfers between devices, extended(): before = lax.ppermute(last, axis, up)  69.9 us
    sub x2, other arithmetic, fluid_update(): center + time_step * (diffusivity * laplace(padded) - advect(padded, velo...  28.9 us
    ppermute x14, starting transfers between devices, extended(): after = lax.ppermute(first, axis, down)  24 us
    scatter-add x1, other arithmetic, body(): heat = jnp.zeros((solid_x * solid_y, row_len), jnp.float32).at[slot_index...  17.6 us
    all_to_all x1, starting transfers between devices, body(): lax.all_to_all(replies, ('gx', 'gy'), split_axis=0, concat_axis=0, tiled=...  17.6 us
    concatenate x11, other arithmetic, extended(): value = jnp.concatenate([before, value, after], axis=dim)  13.6 us
    unnamed x38, local copies, waits for them, and re-layouts  13.4 us
    ppermute x14, waiting for transfers between devices, extended(): after = lax.ppermute(first, axis, down)  12.4 us
  transfers between devices with their start and end apart: 31, of which 3 were waited for; matrix products, arithmetic and copies ran while one was open for 35% of the time, Pallas kernels for 0%

commit v1 on v0

v1 whole, which is shorter than its diff:
```python
import functools

import jax
import jax.numpy as jnp
from jax import lax
from jax.experimental import pallas as pl
from jax.experimental.pallas import tpu as pltpu
from jax.sharding import PartitionSpec as P

MESH = pl.DeviceIdType.MESH
F32 = jnp.float32
BF16 = jnp.bfloat16
I32 = jnp.int32

NGX, NGY = 16, 8
NDEV = 128
CX, CY, NT, LN = 16, 64, 8, 128
SX, SY = 16, 32
CAP = 24
ROWS = 1024
SLOTS = 512
PADY = 8
WT = 5
WH = 4
SP = SX + 2 * WT
SR = 64
R0 = 16
CONDUCT = (0.4, 0.9, 1.5, 2.2)
MODULUS = (0.5, 1.0, 1.6, 2.4)
DIRS = [(dx, dy) for dx in (-1, 0, 1) for dy in (-1, 0, 1) if (dx, dy) != (0, 0)]


def peer_of(gx, gy, k):
    dc, dx, dy, dz = k & 1, (k >> 1) & 3, (k >> 3) & 3, (k >> 5) & 3
    c, z, x, y = gx & 1, gx >> 2, gy & 3, (gx & 2) | (gy >> 2)
    nc, nx, ny, nz = c ^ dc, (x + dx) & 3, (y + dy) & 3, (z + dz) & 3
    return (nz << 2) | (ny & 2) | nc, ((ny & 1) << 2) | nx


def halves(value):
    hi = value.astype(BF16)
    lo = (value - hi.astype(F32)).astype(BF16)
    return jnp.concatenate([hi, lo], axis=1)


def joined(product):
    return product[:, :LN] + product[:, LN:]


def onehot(mask):
    return jnp.where(mask, 1.0, 0.0).astype(BF16)


def lookup(material, table):
    out = jnp.where(material == 0, table[0], 0.0)
    for index in range(1, 4):
        out = jnp.where(material == index, table[index], out)
    return out.astype(F32)


def planes(step, width):
    if step > 0:
        return pl.ds(WT + SX - width, width), pl.ds(WT - width, width)
    if step < 0:
        return pl.ds(WT, width), pl.ds(WT + SX, width)
    return pl.ds(WT, SX), pl.ds(WT, SX)


def lines(step):
    if step > 0:
        return pl.ds(R0 + SY - 8, 8), pl.ds(R0 - 8, 8)
    if step < 0:
        return pl.ds(R0, 8), pl.ds(R0 + SY, 8)
    return pl.ds(R0, SY), pl.ds(R0, SY)


def inside(gx, gy, dx, dy):
    px, py = gx + dx, gy + dy
    return (px >= 0) & (px < NGX) & (py >= 0) & (py < NGY)


def spread_copies(ref, gx, gy, width, sends, recvs):
    out = []
    for i, (dx, dy) in enumerate(DIRS):
        xs, xd = planes(dx, width)
        ys, yd = lines(dy)
        copy = pltpu.make_async_remote_copy(
            src_ref=ref.at[xs, ys, :],
            dst_ref=ref.at[xd, yd, :],
            send_sem=sends.at[i],
            recv_sem=recvs.at[i],
            device_id=(gx + dx, gy + dy),
            device_id_type=MESH,
        )
        out.append((copy, inside(gx, gy, dx, dy), inside(gx, gy, -dx, -dy)))
    return out


def start_all(copies):
    for copy, to, _ in copies:
        pl.when(to)(copy.start)


def wait_recvs(copies):
    for copy, _, came in copies:
        pl.when(came)(copy.wait_recv)


def wait_sends(copies):
    for copy, to, _ in copies:
        pl.when(to)(copy.wait_send)


def face_copies(field, ysend, yrecv, gx, gy, sends, recvs):
    out = []
    rows = pl.ds(PADY, CY)
    for i, step in enumerate((1, -1)):
        src, dst = (CX, 0) if step > 0 else (1, CX + 1)
        copy = pltpu.make_async_remote_copy(
            src_ref=field.at[:, src, rows, :],
            dst_ref=field.at[:, dst, rows, :],
            send_sem=sends.at[i],
            recv_sem=recvs.at[i],
            device_id=(gx + step, gy),
            device_id_type=MESH,
        )
        out.append((copy, inside(gx, gy, step, 0), inside(gx, gy, -step, 0)))
    for i, step in enumerate((1, -1)):
        copy = pltpu.make_async_remote_copy(
            src_ref=ysend.at[i],
            dst_ref=yrecv.at[i],
            send_sem=sends.at[2 + i],
            recv_sem=recvs.at[2 + i],
            device_id=(gx, gy + step),
            device_id_type=MESH,
        )
        out.append((copy, inside(gx, gy, 0, step), inside(gx, gy, 0, -step)))
    return out


def take_faces(field, ysend):
    for t in range(NT):
        ysend[0, t] = field[t, 1 : CX + 1, PADY + CY - 1, :]
        ysend[1, t] = field[t, 1 : CX + 1, PADY, :]


def put_faces(field, yrecv):
    for t in range(NT):
        field[t, 1 : CX + 1, PADY - 1, :] = yrecv[0, t]
        field[t, 1 : CX + 1, PADY + CY, :] = yrecv[1, t]


def fluid_plane(src, dst, vel, flux, x):
    lane = lax.broadcasted_iota(I32, (16, LN), 1)
    first, last = lane == 0, lane == LN - 1
    zero = jnp.zeros((16, LN), F32)
    for h in range(CY // 16):
        r = PADY + 16 * h
        mids = [src[t, x + 1, r : r + 16, :] for t in range(NT)]
        ups = [pltpu.roll(c, LN - 1, 1) for c in mids] + [zero]
        downs = [zero] + [pltpu.roll(c, 1, 1) for c in mids]
        for t in range(NT):
            c = mids[t]
            pairs = (
                (src[t, x + 2, r : r + 16, :], src[t, x, r : r + 16, :]),
                (src[t, x + 1, r + 1 : r + 17, :], src[t, x + 1, r - 1 : r + 15, :]),
                (jnp.where(last, ups[t + 1], ups[t]), jnp.where(first, downs[t], downs[t + 1])),
            )
            total = None
            for k, (p, m) in enumerate(pairs):
                u = vel[k, x, 16 * h : 16 * h + 16, t * LN : (t + 1) * LN].astype(F32)
                a = jnp.maximum(u + 0.5, 0.5)
                pc = p - c
                term = a * ((m - c) + pc) - u * pc
                total = term if total is None else total + term
            if t == 0:
                total = total - flux[pl.ds(pl.multiple_of(x * CY + 16 * h, 16), 16), :]
            dst[t, x + 1, r : r + 16, :] = c + 0.1 * total


def solid_step(src, dst, cond, heat, low, high):
    lane = lax.broadcasted_iota(I32, (SR - 16, LN), 1)

    def one(x, carry):
        c = src[x, 8 : SR - 8, :]
        zp = jnp.where(lane == LN - 1, 0.0, pltpu.roll(c, LN - 1, 1))
        zm = jnp.where(lane == 0, 0.0, pltpu.roll(c, 1, 1))
        beside = src[x + 1, 8 : SR - 8, :] + src[x - 1, 8 : SR - 8, :]
        beside = beside + src[x, 9 : SR - 7, :] + src[x, 7 : SR - 9, :]
        beside = beside + zp + zm
        lap = beside - 6.0 * c
        dst[x, 8 : SR - 8, :] = c + 0.05 * (
            cond[x, 8 : SR - 8, :] * lap + 4.0 * heat[x, 8 : SR - 8, :]
        )
        return carry

    lax.fori_loop(low, high, one, 0)


def kernel(
    fluid_in, vel_in, wall_in, mask_in, owner_in, slot_in, solid_in, mat_in,
    fluid_out, wall_out, solid_out, stress_out,
    f0, f1, vel, wall, mask, flux, owner, slot, dest, dest_s,
    outgoing, incoming, replies, returned, meta_out, meta_in,
    s0, s1, mat, cond, heat, ysend, yrecv,
    in_sem, out_sem, self_sem, a2a_sem, fsend, frecv, ssend, srecv,
):
    gx, gy = lax.axis_index("gx"), lax.axis_index("gy")
    me = gx * NGY + gy

    loads = [
        pltpu.make_async_copy(owner_in, owner, in_sem.at[0]),
        pltpu.make_async_copy(slot_in, slot, in_sem.at[1]),
        pltpu.make_async_copy(wall_in, wall, in_sem.at[2]),
        pltpu.make_async_copy(mask_in, mask, in_sem.at[3]),
    ]
    interior = (pl.ds(1, CX), pl.ds(PADY, CY))
    tiles = [
        pltpu.make_async_copy(
            fluid_in.at[:, :, pl.ds(t * LN, LN)], f0.at[t, interior[0], interior[1], :], in_sem.at[4 + t]
        )
        for t in range(NT)
    ]
    core = (pl.ds(WT, SX), pl.ds(R0, SY))
    load_solid = pltpu.make_async_copy(solid_in, s0.at[core[0], core[1], :], in_sem.at[12])
    load_mat = pltpu.make_async_copy(mat_in, mat.at[core[0], core[1], :], in_sem.at[13])
    load_vel = pltpu.make_async_copy(vel_in, vel, in_sem.at[14])

    for ld in loads[:2]:
        ld.start()
    tiles[0].start()
    for ld in loads[2:]:
        ld.start()

    for field in (f0, f1):
        for t in range(NT):
            for x in (0, CX + 1):
                field[t, x] = jnp.zeros((CY + 2 * PADY, LN), F32)
    yrecv[...] = jnp.zeros_like(yrecv)

    def clear(x, carry):
        for ref, value in ((s0, 0.0), (heat, 0.0), (mat, -1)):
            ref[x, 8:R0, :] = jnp.full((8, LN), value, ref.dtype)
            ref[x, R0 + SY : R0 + SY + 8, :] = jnp.full((8, LN), value, ref.dtype)
        return carry

    lax.fori_loop(0, SP, clear, 0)
    for x in list(range(WT)) + list(range(WT + SX, SP)):
        for ref, value in ((s0, 0.0), (heat, 0.0), (mat, -1)):
            ref[x, R0 : R0 + SY, :] = jnp.full((SY, LN), value, ref.dtype)

    barrier = pltpu.get_barrier_semaphore()

    def greet(k, carry):
        px, py = peer_of(gx, gy, (k * 37) & 127)
        pl.semaphore_signal(barrier, inc=1, device_id=(px, py), device_id_type=MESH)
        return carry

    lax.fori_loop(1, NDEV, greet, 0)
    load_solid.start()
    load_mat.start()
    for t in range(1, NT):
        tiles[t].start()
    load_vel.start()

    loads[0].wait()
    loads[1].wait()
    own_row = owner[...]
    mine = own_row == lax.broadcasted_iota(I32, (NDEV, ROWS), 0)
    mine_b = onehot(mine)
    before = onehot(
        lax.broadcasted_iota(I32, (ROWS, ROWS), 0) < lax.broadcasted_iota(I32, (ROWS, ROWS), 1)
    )
    ranks = jnp.dot(mine_b, before, preferred_element_type=F32)
    rank_row = jnp.sum(jnp.where(mine, ranks, 0.0), axis=0, keepdims=True).astype(I32)
    dest[...] = jnp.clip(own_row * CAP + rank_row, 0, NDEV * CAP - 1)
    place = pltpu.make_async_copy(dest, dest_s, in_sem.at[15])
    place.start()
    code = slot[...] + 1
    at_rank = onehot(rank_row == lax.broadcasted_iota(I32, (LN, ROWS), 0))
    parts = []
    for part in (code & 15, code >> 4):
        left = jnp.where(mine, part.astype(F32), 0.0).astype(BF16)
        parts.append(
            lax.dot_general(left, at_rank, (((1,), (1,)), ((), ())), preferred_element_type=F32)
        )
    meta_out[...] = (parts[0] + 16.0 * parts[1]).reshape(NDEV, 1, LN)

    for ld in loads[2:]:
        ld.wait()
    tiles[0].wait()
    for x in range(CX):
        t0 = f0[0, x + 1, PADY : PADY + CY, :]
        flux[x * CY : (x + 1) * CY, :] = mask[x].astype(F32) * 2.0 * (t0 - wall[x])
    flux_b = halves(flux[...])
    chunk = 16 * CAP

    def pack(i, carry):
        base = pl.multiple_of(i * chunk, chunk)
        pick = onehot(dest[...] == lax.broadcasted_iota(I32, (chunk, ROWS), 0) + base)
        outgoing[pl.ds(base, chunk), :] = joined(jnp.dot(pick, flux_b, preferred_element_type=F32))
        return carry

    lax.fori_loop(0, NDEV // 16, pack, 0)

    pl.semaphore_wait(barrier, NDEV - 1)

    def block(ref, d):
        return ref.at[pl.ds(pl.multiple_of(d * CAP, CAP), CAP), :]

    def send_rows(k, carry):
        px, py = peer_of(gx, gy, (k * 37) & 127)
        other = px * NGY + py
        pltpu.make_async_remote_copy(
            meta_out.at[other], meta_in.at[me], a2a_sem.at[0], a2a_sem.at[1],
            device_id=(px, py), device_id_type=MESH,
        ).start()
        pltpu.make_async_remote_copy(
            block(outgoing, other), block(incoming, me), a2a_sem.at[2], a2a_sem.at[3],
            device_id=(px, py), device_id_type=MESH,
        ).start()
        return carry

    lax.fori_loop(1, NDEV, send_rows, 0)
    own_meta = pltpu.make_async_copy(meta_out.at[me], meta_in.at[me], self_sem.at[0])
    own_rows = pltpu.make_async_copy(block(outgoing, me), block(incoming, me), self_sem.at[1])
    own_meta.start()
    own_rows.start()

    load_solid.wait()
    load_mat.wait()
    temp_copies = spread_copies(s0, gx, gy, WT, ssend.at[0], srecv.at[0])
    mat_copies = spread_copies(mat, gx, gy, WT, ssend.at[1], srecv.at[1])
    start_all(temp_copies)
    start_all(mat_copies)

    for t in range(1, NT):
        tiles[t].wait()
    take_faces(f0, ysend.at[0])
    faces0 = face_copies(f0, ysend.at[0], yrecv.at[0], gx, gy, fsend.at[0], frecv.at[0])
    start_all(faces0)
    load_vel.wait()
    wait_recvs(faces0)
    put_faces(f0, yrecv.at[0])

    def step_one(x, carry):
        fluid_plane(f0, f1, vel, flux, x)
        return carry

    lax.fori_loop(0, CX, step_one, 0)

    take_faces(f1, ysend.at[1])
    faces1 = face_copies(f1, ysend.at[1], yrecv.at[1], gx, gy, fsend.at[1], frecv.at[1])
    start_all(faces1)

    wait_recvs(temp_copies)
    wait_recvs(mat_copies)

    def conduct(x, carry):
        cond[x, 8 : SR - 8, :] = lookup(mat[x, 8 : SR - 8, :], CONDUCT)
        return carry

    lax.fori_loop(0, SP, conduct, 0)

    count = (NDEV - 1) * CAP
    own_meta.wait()
    own_rows.wait()
    pltpu.make_async_copy(meta_in.at[pl.ds(0, NDEV - 1)], meta_in.at[pl.ds(0, NDEV - 1)], a2a_sem.at[1]).wait()
    pltpu.make_async_copy(incoming.at[pl.ds(0, count)], incoming.at[pl.ds(0, count)], a2a_sem.at[3]).wait()
    slots_in = meta_in[...].reshape(NDEV, LN)
    slots_t = slots_in.T
    wanted = lax.broadcasted_iota(I32, (SLOTS, NDEV), 0).astype(F32) + 1.0
    total = jnp.zeros((SLOTS, 2 * LN), F32)
    for k in range(CAP):
        hit = onehot(slots_t[k : k + 1, :] == wanted)
        rows = halves(incoming[pl.ds(k, NDEV, stride=CAP), :])
        total = total + jnp.dot(hit, rows, preferred_element_type=F32)
    heat[WT : WT + SX, R0 : R0 + SY, :] = joined(total).reshape(SX, SY, LN)
    heat_copies = spread_copies(heat, gx, gy, WH, ssend.at[2], srecv.at[2])
    start_all(heat_copies)
    wait_sends(temp_copies)
    wait_sends(mat_copies)
    wait_recvs(heat_copies)

    solid_step(s0, s1, cond, heat, 1, SP - 1)
    solid_step(s1, s0, cond, heat, 2, SP - 2)
    solid_step(s0, s1, cond, heat, 3, SP - 3)
    solid_step(s1, s0, cond, heat, 4, SP - 4)

    done = s0[WT : WT + SX, R0 : R0 + SY, :]
    done_b = halves(done.reshape(SLOTS, LN))
    column = lax.broadcasted_iota(I32, (NDEV, SLOTS), 1).astype(F32) + 1.0
    for k in range(CAP):
        hit = onehot(slots_in[:, k : k + 1] == column)
        replies[pl.ds(k, NDEV, stride=CAP), :] = joined(
            jnp.dot(hit, done_b, preferred_element_type=F32)
        )

    def send_back(k, carry):
        px, py = peer_of(gx, gy, (k * 37) & 127)
        other = px * NGY + py
        pltpu.make_async_remote_copy(
            block(replies, other), block(returned, me), a2a_sem.at[4], a2a_sem.at[5],
            device_id=(px, py), device_id_type=MESH,
        ).start()
        return carry

    lax.fori_loop(1, NDEV, send_back, 0)
    own_back = pltpu.make_async_copy(block(replies, me), block(returned, me), self_sem.at[2])
    own_back.start()

    solid_out[...] = done
    wait_sends(faces0)
    wait_sends(heat_copies)

    def sigma(x, carry):
        s1[x, 8 : SR - 8, :] = lookup(mat[x, 8 : SR - 8, :], MODULUS) * s0[x, 8 : SR - 8, :]
        return carry

    lax.fori_loop(WT - 1, WT + SX + 1, sigma, 0)
    lane = lax.broadcasted_iota(I32, (SY, LN), 1)

    def force(x, carry):
        c = s1[x + WT, R0 : R0 + SY, :]
        zp = jnp.where(lane == LN - 1, 0.0, pltpu.roll(c, LN - 1, 1))
        zm = jnp.where(lane == 0, 0.0, pltpu.roll(c, 1, 1))
        stress_out[0, x] = 0.5 * (
            s1[x + WT + 1, R0 : R0 + SY, :] - s1[x + WT - 1, R0 : R0 + SY, :]
        )
        stress_out[1, x] = 0.5 * (
            s1[x + WT, R0 + 1 : R0 + SY + 1, :] - s1[x + WT, R0 - 1 : R0 + SY - 1, :]
        )
        stress_out[2, x] = 0.5 * (zp - zm)
        return carry

    lax.fori_loop(0, SX, force, 0)

    wait_recvs(faces1)
    put_faces(f1, yrecv.at[1])

    def step_two(x, carry):
        fluid_plane(f1, f0, vel, flux, x)
        return carry

    lax.fori_loop(0, CX, step_two, 0)
    stores = [
        pltpu.make_async_copy(
            f0.at[t, interior[0], interior[1], :], fluid_out.at[:, :, pl.ds(t * LN, LN)], out_sem.at[t]
        )
        for t in range(NT)
    ]
    for st in stores:
        st.start()

    place.wait()
    own_back.wait()
    pltpu.make_async_copy(returned.at[pl.ds(0, count)], returned.at[pl.ds(0, count)], a2a_sem.at[5]).wait()

    def unpack(i, carry):
        for j in range(16):
            r = i * 16 + j
            wall_out[pl.ds(r, 1), :] = returned[pl.ds(dest_s[0, r], 1), :]
        return carry

    lax.fori_loop(0, ROWS // 16, unpack, 0)

    wait_sends(faces1)
    pltpu.make_async_copy(meta_out.at[pl.ds(0, NDEV - 1)], meta_out.at[pl.ds(0, NDEV - 1)], a2a_sem.at[0]).wait()
    pltpu.make_async_copy(outgoing.at[pl.ds(0, count)], outgoing.at[pl.ds(0, count)], a2a_sem.at[2]).wait()
    pltpu.make_async_copy(replies.at[pl.ds(0, count)], replies.at[pl.ds(0, count)], a2a_sem.at[4]).wait()
    for st in stores:
        st.wait()


def body(temp_fluid, velocity, wall_old, wall_mask, owner_map, slot_map, temp_solid, material):
    any_spec = pl.BlockSpec(memory_space=pl.ANY)
    vmem_spec = pl.BlockSpec(memory_space=pltpu.VMEM)
    vm = pltpu.VMEM
    padded = (NT, CX + 2, CY + 2 * PADY, LN)
    dma = pltpu.SemaphoreType.DMA
    fluid, wall, solid, stress = pl.pallas_call(
        kernel,
        out_shape=(
            jax.ShapeDtypeStruct((CX, CY, NT * LN), F32),
            jax.ShapeDtypeStruct((ROWS, LN), F32),
            jax.ShapeDtypeStruct((SX, SY, LN), F32),
            jax.ShapeDtypeStruct((3, SX, SY, LN), F32),
        ),
        in_specs=[any_spec] * 8,
        out_specs=(any_spec, vmem_spec, vmem_spec, vmem_spec),
        scratch_shapes=[
            vm(padded, F32), vm(padded, F32), vm((3, CX, CY, NT * LN), BF16),
            vm((CX, CY, LN), F32), vm((CX, CY, LN), I32), vm((ROWS, LN), F32),
            vm((1, ROWS), I32), vm((1, ROWS), I32), vm((1, ROWS), I32), pltpu.SMEM((1, ROWS), I32),
            vm((NDEV * CAP, LN), F32), vm((NDEV * CAP + CAP, LN), F32),
            vm((NDEV * CAP + CAP, LN), F32), vm((NDEV * CAP, LN), F32),
            vm((NDEV, 1, LN), F32), vm((NDEV, 1, LN), F32),
            vm((SP, SR, LN), F32), vm((SP, SR, LN), F32), vm((SP, SR, LN), I32),
            vm((SP, SR, LN), F32), vm((SP, SR, LN), F32),
            vm((2, 2, NT, CX, LN), F32), vm((2, 2, NT, CX, LN), F32),
            dma((16,)), dma((NT,)), dma((3,)), dma((6,)),
            dma((2, 4)), dma((2, 4)), dma((3, 8)), dma((3, 8)),
        ],
        compiler_params=pltpu.CompilerParams(
            collective_id=0, has_side_effects=True, vmem_limit_bytes=60 * 1024 * 1024
        ),
    )(
        temp_fluid, velocity, wall_old, wall_mask,
        owner_map.reshape(1, ROWS), slot_map, temp_solid, material,
    )
    return fluid, wall.reshape(CX, CY, LN), solid, stress


def solution(mesh):
    placed = (
        P("gx", "gy", None),
        P(None, "gx", "gy", None),
        P("gx", "gy", None),
        P("gx", "gy", None),
        P(("gx", "gy"), None, None),
        P(("gx", "gy"), None),
        P("gx", "gy", None),
        P("gx", "gy", None),
    )
    return jax.shard_map(
        body,
        mesh=mesh,
        in_specs=placed,
        out_specs=(
            P("gx", "gy", None),
            P("gx", "gy", None),
            P("gx", "gy", None),
            P(None, "gx", "gy", None),
        ),
        check_vma=False,
    )
```

time: 256 us -> 105 us (0.41)
  starting transfers between devices: 132 us -> 0 us
  Pallas kernels: 0 us -> 97 us
  other arithmetic: 66 us -> 0 us
  local copies, waits for them, and re-layouts: 40.1 us -> 7.29 us
  waiting for transfers between devices: 13.7 us -> 0 us
    pallas_call x0 -> x1, Pallas kernels: none -> 97 us  [body(): pl.pallas_call(kernel, out_shape=(jax.ShapeDtypeStruct((CX, CY, NT * LN),...]
    ppermute x28 -> x0, starting transfers between devices: 93.9 us -> none  [the longest x14 69.9 us: extended(): before = lax.ppermute(last, axis, up)]
    all_to_all x3 -> x0, starting transfers between devices: 38.2 us -> none  [the longest x1 17.6 us: body(): lax.all_to_all(replies, ('gx', 'gy'), split_axis=0, concat_axis=0, tiled=...]
    sub x3 -> x0, other arithmetic: 29 us -> none  [the longest x2 28.9 us: fluid_update(): center + time_step * (diffusivity * laplace(padded) - advect(padded, velo...]
    gather x2 -> x0, local copies, waits for them, and re-layouts: 22.4 us -> none  [the longest x1 11.6 us: body(): wall_next = returned[owner, position].reshape(cells_x, cells_y, row_len)]
    scatter-add x1 -> x0, other arithmetic: 17.6 us -> none  [body(): heat = jnp.zeros((solid_x * solid_y, row_len), jnp.float32).at[slot_index...]
    ppermute x28 -> x0, waiting for transfers between devices: 13.7 us -> none  [the longest x14 12.4 us: extended(): after = lax.ppermute(first, axis, down)]
    concatenate x12 -> x0, other arithmetic: 13.7 us -> none  [the longest x11 13.6 us: extended(): value = jnp.concatenate([before, value, after], axis=dim)]
  transfers between devices with their start and end apart: 31 -> 0, of which waited for: 3 -> 0; matrix products, arithmetic and copies ran while one was open for 35% -> 0% of each run, Pallas kernels for 0% -> 0%
where the time goes in v1:
time: 105 us
  Pallas kernels  97 us (92%)
  local copies, waits for them, and re-layouts  7.29 us (7%)
    pallas_call x1, Pallas kernels, body(): pl.pallas_call(kernel, out_shape=(jax.ShapeDtypeStruct((CX, CY, NT * LN),...  97 us
    unnamed x10, local copies, waits for them, and re-layouts  7.29 us

profile of v1, /device:TPU:1, one launch (start us, length us, event | category | flops | bytes accessed | tf_op | source)
XLA Modules:
  0.0 104.9 jit_solution(6627184965665764998)
XLA Ops:
  0.6 97.0 %shard_map.111 = (f32[16,64,1024]{2,1,0:T(8,128)}, f32[1024,128]{1,0:T(8,128)}, f32[16,32,128]{2,1,0:T(8,128)}, f32[3,16,32,128]{3,2,1,0:T(8,128)}) custom-call(f32[16,64,1024]{2,1,0:T(8,128)} %fluid_in.1, bf16[3,16,64,1024]{3,2,1,0:T(8,128)(2,1)} %vel_in.1, f32[16,64,128]{2,1,0:T(8,128)} %wall_in.1, s32[16,64,128]{2,1,0:T(8,128)} %mask_in.1, ...), custom_call_target="tpu_custom_call" | custom-call | tf_op jit(solution)/shard_map/pallas_call | solution.py:481
  97.6 0.0 copy-start.1
  97.6 0.0 copy-start.2
  97.6 0.0 copy-start
  97.6 4.9 %copy.16 = f32[16,64,1024]{2,1,0:T(8,128)} copy(f32[16,64,1024]{2,1,0:T(8,128)} %get-tuple-element.16) | data formatting | bytes 8388608
  102.5 0.0 copy-done.1
  102.5 0.8 copy.17
  103.3 0.0 copy-done.2
  103.3 0.7 copy.18
  104.0 0.0 copy-done
  104.0 0.9 copy.19
Async XLA Ops:
  97.6 4.9 %copy-start.1 = (f32[1024,128]{1,0:T(8,128)S(1)}, f32[1024,128]{1,0:T(8,128)}, u32[]{:S(2)}) copy-start(f32[1024,128]{1,0:T(8,128)} %get-tuple-element.9) | copy-start | bytes 1572868
  97.6 5.7 %copy-start.2 = (f32[16,32,128]{2,1,0:T(8,128)S(1)}, f32[16,32,128]{2,1,0:T(8,128)}, u32[]{:S(2)}) copy-start(f32[16,32,128]{2,1,0:T(8,128)} %get-tuple-element.18) | copy-start | bytes 786436
  97.6 6.4 %copy-start = (f32[3,16,32,128]{3,2,1,0:T(8,128)S(1)}, f32[3,16,32,128]{3,2,1,0:T(8,128)}, u32[]{:S(2)}) copy-start(f32[3,16,32,128]{3,2,1,0:T(8,128)} %get-tuple-element.19) | copy-start | bytes 2359300

commit v2 on v1

--- a/solution.py
+++ b/solution.py
@@ -25,7 +25,7 @@
 SP = SX + 2 * WT
 SR = 64
 R0 = 16
-CONDUCT = (0.4, 0.9, 1.5, 2.2)
+CONDUCT = (0.05 * 0.4, 0.05 * 0.9, 0.05 * 1.5, 0.05 * 2.2)
 MODULUS = (0.5, 1.0, 1.6, 2.4)
 DIRS = [(dx, dy) for dx in (-1, 0, 1) for dy in (-1, 0, 1) if (dx, dy) != (0, 0)]
 
@@ -150,7 +150,7 @@
         field[t, 1 : CX + 1, PADY + CY, :] = yrecv[1, t]
 
 
-def fluid_plane(src, dst, vel, flux, x):
+def fluid_plane(src, put, vel, flux, x):
     lane = lax.broadcasted_iota(I32, (16, LN), 1)
     first, last = lane == 0, lane == LN - 1
     zero = jnp.zeros((16, LN), F32)
@@ -175,26 +175,20 @@
                 total = term if total is None else total + term
             if t == 0:
                 total = total - flux[pl.ds(pl.multiple_of(x * CY + 16 * h, 16), 16), :]
-            dst[t, x + 1, r : r + 16, :] = c + 0.1 * total
-
-
-def solid_step(src, dst, cond, heat, low, high):
+            put(t, x, h, c + 0.1 * total)
+
+
+def solid_step(src, dst, cond, heat):
     lane = lax.broadcasted_iota(I32, (SR - 16, LN), 1)
-
-    def one(x, carry):
+    last, first = lane == LN - 1, lane == 0
+    for x in range(1, SP - 1):
         c = src[x, 8 : SR - 8, :]
-        zp = jnp.where(lane == LN - 1, 0.0, pltpu.roll(c, LN - 1, 1))
-        zm = jnp.where(lane == 0, 0.0, pltpu.roll(c, 1, 1))
+        zp = jnp.where(last, 0.0, pltpu.roll(c, LN - 1, 1))
+        zm = jnp.where(first, 0.0, pltpu.roll(c, 1, 1))
         beside = src[x + 1, 8 : SR - 8, :] + src[x - 1, 8 : SR - 8, :]
-        beside = beside + src[x, 9 : SR - 7, :] + src[x, 7 : SR - 9, :]
-        beside = beside + zp + zm
-        lap = beside - 6.0 * c
-        dst[x, 8 : SR - 8, :] = c + 0.05 * (
-            cond[x, 8 : SR - 8, :] * lap + 4.0 * heat[x, 8 : SR - 8, :]
-        )
-        return carry
-
-    lax.fori_loop(low, high, one, 0)
+        beside = beside + (src[x, 9 : SR - 7, :] + src[x, 7 : SR - 9, :])
+        lap = beside + (zp + zm) - 6.0 * c
+        dst[x, 8 : SR - 8, :] = c + (cond[x, 8 : SR - 8, :] * lap + 0.2 * heat[x, 8 : SR - 8, :])
 
 
 def kernel(
@@ -203,7 +197,7 @@
     f0, f1, vel, wall, mask, flux, owner, slot, dest, dest_s,
     outgoing, incoming, replies, returned, meta_out, meta_in,
     s0, s1, mat, cond, heat, ysend, yrecv,
-    in_sem, out_sem, self_sem, a2a_sem, fsend, frecv, ssend, srecv,
+    in_sem, self_sem, a2a_sem, fsend, frecv, ssend, srecv,
 ):
     gx, gy = lax.axis_index("gx"), lax.axis_index("gy")
     me = gx * NGY + gy
@@ -303,7 +297,12 @@
 
     lax.fori_loop(0, NDEV // 16, pack, 0)
 
+    for t in range(1, NT):
+        tiles[t].wait()
+    take_faces(f0, ysend.at[0])
+    faces0 = face_copies(f0, ysend.at[0], yrecv.at[0], gx, gy, fsend.at[0], frecv.at[0])
     pl.semaphore_wait(barrier, NDEV - 1)
+    start_all(faces0)
 
     def block(ref, d):
         return ref.at[pl.ds(pl.multiple_of(d * CAP, CAP), CAP), :]
@@ -334,47 +333,50 @@
     start_all(temp_copies)
     start_all(mat_copies)
 
-    for t in range(1, NT):
-        tiles[t].wait()
-    take_faces(f0, ysend.at[0])
-    faces0 = face_copies(f0, ysend.at[0], yrecv.at[0], gx, gy, fsend.at[0], frecv.at[0])
-    start_all(faces0)
     load_vel.wait()
     wait_recvs(faces0)
     put_faces(f0, yrecv.at[0])
 
+    def keep(t, x, h, value):
+        f1[t, x + 1, PADY + 16 * h : PADY + 16 * h + 16, :] = value
+
     def step_one(x, carry):
-        fluid_plane(f0, f1, vel, flux, x)
+        fluid_plane(f0, keep, vel, flux, x)
         return carry
 
     lax.fori_loop(0, CX, step_one, 0)
 
     take_faces(f1, ysend.at[1])
     faces1 = face_copies(f1, ysend.at[1], yrecv.at[1], gx, gy, fsend.at[1], frecv.at[1])
-    start_all(faces1)
 
     wait_recvs(temp_copies)
     wait_recvs(mat_copies)
 
     def conduct(x, carry):
-        cond[x, 8 : SR - 8, :] = lookup(mat[x, 8 : SR - 8, :], CONDUCT)
-        return carry
-
-    lax.fori_loop(0, SP, conduct, 0)
+        for j in range(2):
+            cond[2 * x + j, 8 : SR - 8, :] = lookup(mat[2 * x + j, 8 : SR - 8, :], CONDUCT)
+        return carry
+
+    lax.fori_loop(0, SP // 2, conduct, 0)
 
     count = (NDEV - 1) * CAP
     own_meta.wait()
     own_rows.wait()
     pltpu.make_async_copy(meta_in.at[pl.ds(0, NDEV - 1)], meta_in.at[pl.ds(0, NDEV - 1)], a2a_sem.at[1]).wait()
     pltpu.make_async_copy(incoming.at[pl.ds(0, count)], incoming.at[pl.ds(0, count)], a2a_sem.at[3]).wait()
+    start_all(faces1)
     slots_in = meta_in[...].reshape(NDEV, LN)
     slots_t = slots_in.T
     wanted = lax.broadcasted_iota(I32, (SLOTS, NDEV), 0).astype(F32) + 1.0
-    total = jnp.zeros((SLOTS, 2 * LN), F32)
-    for k in range(CAP):
-        hit = onehot(slots_t[k : k + 1, :] == wanted)
-        rows = halves(incoming[pl.ds(k, NDEV, stride=CAP), :])
-        total = total + jnp.dot(hit, rows, preferred_element_type=F32)
+    total = None
+    for first in range(0, CAP, 6):
+        span = range(first, first + 6)
+        hits = jnp.concatenate([onehot(slots_t[k : k + 1, :] == wanted) for k in span], axis=1)
+        rows = jnp.concatenate(
+            [halves(incoming[pl.ds(k, NDEV, stride=CAP), :]) for k in span], axis=0
+        )
+        some = jnp.dot(hits, rows, preferred_element_type=F32)
+        total = some if total is None else total + some
     heat[WT : WT + SX, R0 : R0 + SY, :] = joined(total).reshape(SX, SY, LN)
     heat_copies = spread_copies(heat, gx, gy, WH, ssend.at[2], srecv.at[2])
     start_all(heat_copies)
@@ -382,30 +384,36 @@
     wait_sends(mat_copies)
     wait_recvs(heat_copies)
 
-    solid_step(s0, s1, cond, heat, 1, SP - 1)
-    solid_step(s1, s0, cond, heat, 2, SP - 2)
-    solid_step(s0, s1, cond, heat, 3, SP - 3)
-    solid_step(s1, s0, cond, heat, 4, SP - 4)
+    solid_step(s0, s1, cond, heat)
+    solid_step(s1, s0, cond, heat)
+    solid_step(s0, s1, cond, heat)
+    solid_step(s1, s0, cond, heat)
 
     done = s0[WT : WT + SX, R0 : R0 + SY, :]
     done_b = halves(done.reshape(SLOTS, LN))
-    column = lax.broadcasted_iota(I32, (NDEV, SLOTS), 1).astype(F32) + 1.0
-    for k in range(CAP):
-        hit = onehot(slots_in[:, k : k + 1] == column)
-        replies[pl.ds(k, NDEV, stride=CAP), :] = joined(
-            jnp.dot(hit, done_b, preferred_element_type=F32)
-        )
-
-    def send_back(k, carry):
-        px, py = peer_of(gx, gy, (k * 37) & 127)
-        other = px * NGY + py
-        pltpu.make_async_remote_copy(
-            block(replies, other), block(returned, me), a2a_sem.at[4], a2a_sem.at[5],
-            device_id=(px, py), device_id_type=MESH,
-        ).start()
-        return carry
-
-    lax.fori_loop(1, NDEV, send_back, 0)
+    part = NDEV // 4
+    column = lax.broadcasted_iota(I32, (part, SLOTS), 1).astype(F32) + 1.0
+    for q in range(4):
+        dz = (gx >> 2) + q
+        first = pl.multiple_of((dz & 3) * part, part)
+        some_slots = meta_in[pl.ds(first, part)].reshape(part, LN)
+        hits = jnp.concatenate(
+            [onehot(some_slots[:, k : k + 1] == column) for k in range(CAP)], axis=0
+        )
+        picked = joined(jnp.dot(hits, done_b, preferred_element_type=F32))
+        for k in range(CAP):
+            replies[pl.ds(first * CAP + k, part, stride=CAP), :] = picked[k * part : (k + 1) * part]
+
+        def send_back(k, carry):
+            px, py = peer_of(gx, gy, q * 32 + ((k * 13) & 31))
+            other = px * NGY + py
+            pltpu.make_async_remote_copy(
+                block(replies, other), block(returned, me), a2a_sem.at[4], a2a_sem.at[5],
+                device_id=(px, py), device_id_type=MESH,
+            ).start()
+            return carry
+
+        lax.fori_loop(1 if q == 0 else 0, 32, send_back, 0)
     own_back = pltpu.make_async_copy(block(replies, me), block(returned, me), self_sem.at[2])
     own_back.start()
 
@@ -414,10 +422,12 @@
     wait_sends(heat_copies)
 
     def sigma(x, carry):
-        s1[x, 8 : SR - 8, :] = lookup(mat[x, 8 : SR - 8, :], MODULUS) * s0[x, 8 : SR - 8, :]
-        return carry
-
-    lax.fori_loop(WT - 1, WT + SX + 1, sigma, 0)
+        for j in range(2):
+            y = WT - 1 + 2 * x + j
+            s1[y, 8 : SR - 8, :] = lookup(mat[y, 8 : SR - 8, :], MODULUS) * s0[y, 8 : SR - 8, :]
+        return carry
+
+    lax.fori_loop(0, SX // 2 + 1, sigma, 0)
     lane = lax.broadcasted_iota(I32, (SY, LN), 1)
 
     def force(x, carry):
@@ -438,19 +448,14 @@
     wait_recvs(faces1)
     put_faces(f1, yrecv.at[1])
 
+    def give(t, x, h, value):
+        fluid_out[x, 16 * h : 16 * h + 16, t * LN : (t + 1) * LN] = value
+
     def step_two(x, carry):
-        fluid_plane(f1, f0, vel, flux, x)
+        fluid_plane(f1, give, vel, flux, x)
         return carry
 
     lax.fori_loop(0, CX, step_two, 0)
-    stores = [
-        pltpu.make_async_copy(
-            f0.at[t, interior[0], interior[1], :], fluid_out.at[:, :, pl.ds(t * LN, LN)], out_sem.at[t]
-        )
-        for t in range(NT)
-    ]
-    for st in stores:
-        st.start()
 
     place.wait()
     own_back.wait()
@@ -468,12 +473,19 @@
     pltpu.make_async_copy(meta_out.at[pl.ds(0, NDEV - 1)], meta_out.at[pl.ds(0, NDEV - 1)], a2a_sem.at[0]).wait()
     pltpu.make_async_copy(outgoing.at[pl.ds(0, count)], outgoing.at[pl.ds(0, count)], a2a_sem.at[2]).wait()
     pltpu.make_async_copy(replies.at[pl.ds(0, count)], replies.at[pl.ds(0, count)], a2a_sem.at[4]).wait()
-    for st in stores:
-        st.wait()
+
+
+def store(*refs):
+    sems = refs[-1]
+    copies = [pltpu.make_async_copy(refs[i], refs[4 + i], sems.at[i]) for i in range(4)]
+    for copy in copies:
+        copy.start()
+    for copy in copies:
+        copy.wait()
 
 
 def body(temp_fluid, velocity, wall_old, wall_mask, owner_map, slot_map, temp_solid, material):
-    any_spec = pl.BlockSpec(memory_space=pl.ANY)
+    hbm_spec = pl.BlockSpec(memory_space=pltpu.HBM)
     vmem_spec = pl.BlockSpec(memory_space=pltpu.VMEM)
     vm = pltpu.VMEM
     padded = (NT, CX + 2, CY + 2 * PADY, LN)
@@ -486,8 +498,8 @@
             jax.ShapeDtypeStruct((SX, SY, LN), F32),
             jax.ShapeDtypeStruct((3, SX, SY, LN), F32),
         ),
-        in_specs=[any_spec] * 8,
-        out_specs=(any_spec, vmem_spec, vmem_spec, vmem_spec),
+        in_specs=[hbm_spec] * 8,
+        out_specs=(vmem_spec,) * 4,
         scratch_shapes=[
             vm(padded, F32), vm(padded, F32), vm((3, CX, CY, NT * LN), BF16),
             vm((CX, CY, LN), F32), vm((CX, CY, LN), I32), vm((ROWS, LN), F32),
@@ -498,17 +510,26 @@
             vm((SP, SR, LN), F32), vm((SP, SR, LN), F32), vm((SP, SR, LN), I32),
             vm((SP, SR, LN), F32), vm((SP, SR, LN), F32),
             vm((2, 2, NT, CX, LN), F32), vm((2, 2, NT, CX, LN), F32),
-            dma((16,)), dma((NT,)), dma((3,)), dma((6,)),
+            dma((16,)), dma((3,)), dma((10,)),
             dma((2, 4)), dma((2, 4)), dma((3, 8)), dma((3, 8)),
         ],
         compiler_params=pltpu.CompilerParams(
-            collective_id=0, has_side_effects=True, vmem_limit_bytes=60 * 1024 * 1024
+            collective_id=0, has_side_effects=True, vmem_limit_bytes=40 * 1024 * 1024
         ),
-    )(
-        temp_fluid, velocity, wall_old, wall_mask,
-        owner_map.reshape(1, ROWS), slot_map, temp_solid, material,
-    )
-    return fluid, wall.reshape(CX, CY, LN), solid, stress
+    )(*[
+        pltpu.with_memory_space_constraint(x, pltpu.HBM)
+        for x in (temp_fluid, velocity, wall_old, wall_mask,
+        owner_map.reshape(1, ROWS), slot_map, temp_solid, material)
+    ])
+    results = (fluid, wall.reshape(CX, CY, LN), solid, stress)
+    return pl.pallas_call(
+        store,
+        out_shape=tuple(jax.ShapeDtypeStruct(r.shape, F32) for r in results),
+        in_specs=[pl.BlockSpec(memory_space=pl.ANY)] * 4,
+        out_specs=(pl.BlockSpec(memory_space=pl.ANY),) * 4,
+        scratch_shapes=[dma((4,))],
+        compiler_params=pltpu.CompilerParams(vmem_limit_bytes=1024 * 1024),
+    )(*results)
 
 
 def solution(mesh):

time: 105 us -> 89.2 us (0.85)
  Pallas kernels: 97 us -> 88.5 us
  local copies, waits for them, and re-layouts: 7.29 us -> 0 us
    pallas_call x1, Pallas kernels: 97 us -> 86 us  [body(): pl.pallas_call(kernel, out_shape=(jax.ShapeDtypeStruct((CX, CY, NT * LN),...]
    unnamed x10 -> x0, local copies, waits for them, and re-layouts: 7.29 us -> none
    pallas_call x0 -> x1, Pallas kernels: none -> 2.53 us  [body(): pl.pallas_call(store, out_shape=tuple((jax.ShapeDtypeStruct(r.shape, F32)...]
where the time goes in v2:
time: 89.2 us; the launch traced here: 89.1 us
  Pallas kernels  88.5 us (99%)
    pallas_call x1, Pallas kernels, body(): pl.pallas_call(kernel, out_shape=(jax.ShapeDtypeStruct((CX, CY, NT * LN),...  86 us
    pallas_call x1, Pallas kernels, body(): pl.pallas_call(store, out_shape=tuple((jax.ShapeDtypeStruct(r.shape, F32)...  2.53 us

profile of v2, /device:TPU:1, one launch (start us, length us, event | category | flops | bytes accessed | tf_op | source)
XLA Modules:
  0.0 89.1 jit_solution(15982857719690627639)
XLA Ops:
  0.6 86.0 %shard_map.111 = (f32[16,64,1024]{2,1,0:T(8,128)S(1)}, f32[1024,128]{1,0:T(8,128)S(1)}, f32[16,32,128]{2,1,0:T(8,128)S(1)}, f32[3,16,32,128]{3,2,1,0:T(8,128)S(1)}) custom-call(f32[16,64,1024]{2,1,0:T(8,128)} %fluid_in.1, bf16[3,16,64,1024]{3,2,1,0:T(8,128)(2,1)} %vel_in.1, f32[16,64,128]{2,1,0:T(8,128)} %wall_in.1, s32[16,64,128]{2,1,0:T(8,128)} %mask_in.1, ...), custom_call_target="tpu_custom_call" | custom-call | tf_op jit(solution)/shard_map/pallas_call | solution.py:493
  86.6 2.5 %shard_map.112 = (f32[16,64,1024]{2,1,0:T(8,128)}, f32[16,64,128]{2,1,0:T(8,128)}, f32[16,32,128]{2,1,0:T(8,128)}, f32[3,16,32,128]{3,2,1,0:T(8,128)}) custom-call(f32[16,64,1024]{2,1,0:T(8,128)S(1)} %get-tuple-element.8.refs_0_, f32[16,64,128]{2,1,0:T(8,128)S(1)} %bitcast.2, f32[16,32,128]{2,1,0:T(8,128)S(1)} %get-tuple-element.10.refs_2_, ...), custom_call_target="tpu_custom_call" | custom-call | tf_op jit(solution)/shard_map/pallas_call | solution.py:525

commit v3 on v2

--- a/solution.py
+++ b/solution.py
@@ -82,7 +82,7 @@
 def spread_copies(ref, gx, gy, width, sends, recvs):
     out = []
     for i, (dx, dy) in enumerate(DIRS):
-        xs, xd = planes(dx, width)
+        xs, xd = planes(dx, width - 1 if dy else width)
         ys, yd = lines(dy)
         copy = pltpu.make_async_remote_copy(
             src_ref=ref.at[xs, ys, :],
@@ -329,7 +329,7 @@
     load_solid.wait()
     load_mat.wait()
     temp_copies = spread_copies(s0, gx, gy, WT, ssend.at[0], srecv.at[0])
-    mat_copies = spread_copies(mat, gx, gy, WT, ssend.at[1], srecv.at[1])
+    mat_copies = spread_copies(mat, gx, gy, WH, ssend.at[1], srecv.at[1])
     start_all(temp_copies)
     start_all(mat_copies)
 
@@ -348,23 +348,12 @@
 
     take_faces(f1, ysend.at[1])
     faces1 = face_copies(f1, ysend.at[1], yrecv.at[1], gx, gy, fsend.at[1], frecv.at[1])
-
-    wait_recvs(temp_copies)
-    wait_recvs(mat_copies)
-
-    def conduct(x, carry):
-        for j in range(2):
-            cond[2 * x + j, 8 : SR - 8, :] = lookup(mat[2 * x + j, 8 : SR - 8, :], CONDUCT)
-        return carry
-
-    lax.fori_loop(0, SP // 2, conduct, 0)
 
     count = (NDEV - 1) * CAP
     own_meta.wait()
     own_rows.wait()
     pltpu.make_async_copy(meta_in.at[pl.ds(0, NDEV - 1)], meta_in.at[pl.ds(0, NDEV - 1)], a2a_sem.at[1]).wait()
     pltpu.make_async_copy(incoming.at[pl.ds(0, count)], incoming.at[pl.ds(0, count)], a2a_sem.at[3]).wait()
-    start_all(faces1)
     slots_in = meta_in[...].reshape(NDEV, LN)
     slots_t = slots_in.T
     wanted = lax.broadcasted_iota(I32, (SLOTS, NDEV), 0).astype(F32) + 1.0
@@ -380,6 +369,17 @@
     heat[WT : WT + SX, R0 : R0 + SY, :] = joined(total).reshape(SX, SY, LN)
     heat_copies = spread_copies(heat, gx, gy, WH, ssend.at[2], srecv.at[2])
     start_all(heat_copies)
+    start_all(faces1)
+    wait_recvs(temp_copies)
+    wait_recvs(mat_copies)
+
+    def conduct(x, carry):
+        for j in range(2):
+            cond[2 * x + j, 8 : SR - 8, :] = lookup(mat[2 * x + j, 8 : SR - 8, :], CONDUCT)
+        return carry
+
+    lax.fori_loop(0, SP // 2, conduct, 0)
+
     wait_sends(temp_copies)
     wait_sends(mat_copies)
     wait_recvs(heat_copies)
@@ -391,21 +391,24 @@
 
     done = s0[WT : WT + SX, R0 : R0 + SY, :]
     done_b = halves(done.reshape(SLOTS, LN))
-    part = NDEV // 4
-    column = lax.broadcasted_iota(I32, (part, SLOTS), 1).astype(F32) + 1.0
-    for q in range(4):
-        dz = (gx >> 2) + q
-        first = pl.multiple_of((dz & 3) * part, part)
-        some_slots = meta_in[pl.ds(first, part)].reshape(part, LN)
+    column = lax.broadcasted_iota(I32, (NDEV // 2, SLOTS), 1).astype(F32) + 1.0
+    for core in range(2):
+        starts = [(2 * g + core) * NGY for g in range(NGX // 2)]
+        some_slots = jnp.concatenate(
+            [meta_in[b : b + NGY].reshape(NGY, LN) for b in starts], axis=0
+        )
         hits = jnp.concatenate(
             [onehot(some_slots[:, k : k + 1] == column) for k in range(CAP)], axis=0
         )
         picked = joined(jnp.dot(hits, done_b, preferred_element_type=F32))
         for k in range(CAP):
-            replies[pl.ds(first * CAP + k, part, stride=CAP), :] = picked[k * part : (k + 1) * part]
-
-        def send_back(k, carry):
-            px, py = peer_of(gx, gy, q * 32 + ((k * 13) & 31))
+            for g, b in enumerate(starts):
+                r = k * (NDEV // 2) + g * NGY
+                replies[pl.ds(b * CAP + k, NGY, stride=CAP), :] = picked[r : r + NGY]
+        flip = (gx & 1) ^ core
+
+        def send_back(j, carry):
+            px, py = peer_of(gx, gy, 2 * ((j * 37) & 63) + flip)
             other = px * NGY + py
             pltpu.make_async_remote_copy(
                 block(replies, other), block(returned, me), a2a_sem.at[4], a2a_sem.at[5],
@@ -413,7 +416,7 @@
             ).start()
             return carry
 
-        lax.fori_loop(1 if q == 0 else 0, 32, send_back, 0)
+        lax.fori_loop(1 - flip, NDEV // 2, send_back, 0)
     own_back = pltpu.make_async_copy(block(replies, me), block(returned, me), self_sem.at[2])
     own_back.start()
 

time: 89.2 us -> 81.9 us (0.918)
  Pallas kernels: 88.5 us -> 81 us
    pallas_call x1, Pallas kernels: 86 us -> 78.4 us  [body(): pl.pallas_call(kernel, out_shape=(jax.ShapeDtypeStruct((CX, CY, NT * LN),...]
where the time goes in v3:
time: 81.9 us; the launch traced here: 81.6 us
  Pallas kernels  81 us (99%)
    pallas_call x1, Pallas kernels, body(): pl.pallas_call(kernel, out_shape=(jax.ShapeDtypeStruct((CX, CY, NT * LN),...  78.4 us
    pallas_call x1, Pallas kernels, body(): pl.pallas_call(store, out_shape=tuple((jax.ShapeDtypeStruct(r.shape, F32)...  2.53 us

profile of v3, /device:TPU:1, one launch (start us, length us, event | category | flops | bytes accessed | tf_op | source)
XLA Modules:
  0.0 81.6 jit_solution(6061649306140404658)
XLA Ops:
  0.6 78.4 %shard_map.111 = (f32[16,64,1024]{2,1,0:T(8,128)S(1)}, f32[1024,128]{1,0:T(8,128)S(1)}, f32[16,32,128]{2,1,0:T(8,128)S(1)}, f32[3,16,32,128]{3,2,1,0:T(8,128)S(1)}) custom-call(f32[16,64,1024]{2,1,0:T(8,128)} %fluid_in.1, bf16[3,16,64,1024]{3,2,1,0:T(8,128)(2,1)} %vel_in.1, f32[16,64,128]{2,1,0:T(8,128)} %wall_in.1, s32[16,64,128]{2,1,0:T(8,128)} %mask_in.1, ...), custom_call_target="tpu_custom_call" | custom-call | tf_op jit(solution)/shard_map/pallas_call | solution.py:496
  79.1 2.5 %shard_map.112 = (f32[16,64,1024]{2,1,0:T(8,128)}, f32[16,64,128]{2,1,0:T(8,128)}, f32[16,32,128]{2,1,0:T(8,128)}, f32[3,16,32,128]{3,2,1,0:T(8,128)}) custom-call(f32[16,64,1024]{2,1,0:T(8,128)S(1)} %get-tuple-element.8.refs_0_, f32[16,64,128]{2,1,0:T(8,128)S(1)} %bitcast.2, f32[16,32,128]{2,1,0:T(8,128)S(1)} %get-tuple-element.10.refs_2_, ...), custom_call_target="tpu_custom_call" | custom-call | tf_op jit(solution)/shard_map/pallas_call | solution.py:528

commit v4 on v3

--- a/solution.py
+++ b/solution.py
@@ -178,10 +178,10 @@
             put(t, x, h, c + 0.1 * total)
 
 
-def solid_step(src, dst, cond, heat):
+def solid_step(src, dst, cond, heat, edge):
     lane = lax.broadcasted_iota(I32, (SR - 16, LN), 1)
     last, first = lane == LN - 1, lane == 0
-    for x in range(1, SP - 1):
+    for x in range(edge, SP - edge):
         c = src[x, 8 : SR - 8, :]
         zp = jnp.where(last, 0.0, pltpu.roll(c, LN - 1, 1))
         zm = jnp.where(first, 0.0, pltpu.roll(c, 1, 1))
@@ -226,23 +226,6 @@
     for ld in loads[2:]:
         ld.start()
 
-    for field in (f0, f1):
-        for t in range(NT):
-            for x in (0, CX + 1):
-                field[t, x] = jnp.zeros((CY + 2 * PADY, LN), F32)
-    yrecv[...] = jnp.zeros_like(yrecv)
-
-    def clear(x, carry):
-        for ref, value in ((s0, 0.0), (heat, 0.0), (mat, -1)):
-            ref[x, 8:R0, :] = jnp.full((8, LN), value, ref.dtype)
-            ref[x, R0 + SY : R0 + SY + 8, :] = jnp.full((8, LN), value, ref.dtype)
-        return carry
-
-    lax.fori_loop(0, SP, clear, 0)
-    for x in list(range(WT)) + list(range(WT + SX, SP)):
-        for ref, value in ((s0, 0.0), (heat, 0.0), (mat, -1)):
-            ref[x, R0 : R0 + SY, :] = jnp.full((SY, LN), value, ref.dtype)
-
     barrier = pltpu.get_barrier_semaphore()
 
     def greet(k, carry):
@@ -256,6 +239,33 @@
     for t in range(1, NT):
         tiles[t].start()
     load_vel.start()
+
+
+    def beyond(first, count, low, high):
+        def clear(x, carry):
+            for ref, value in ((s0, 0.0), (heat, 0.0), (mat, -1)):
+                ref[first + x, low:high, :] = jnp.full((high - low, LN), value, ref.dtype)
+            return carry
+
+        lax.fori_loop(0, count, clear, 0)
+
+    for side, at_edge in ((0, gx == 0), (1, gx == NGX - 1)):
+
+        @pl.when(at_edge)
+        def _(side=side):
+            for field in (f0, f1):
+                for t in range(NT):
+                    field[t, side * (CX + 1)] = jnp.zeros((CY + 2 * PADY, LN), F32)
+            beyond(side * (WT + SX), WT, 8, SR - 8)
+
+    for side, at_edge in ((0, gy == 0), (1, gy == NGY - 1)):
+
+        @pl.when(at_edge)
+        def _(side=side):
+            for turn in range(2):
+                yrecv[turn, side] = jnp.zeros((NT, CX, LN), F32)
+            low = R0 - 8 + side * (SY + 8)
+            beyond(0, SP, low, low + 8)
 
     loads[0].wait()
     loads[1].wait()
@@ -302,7 +312,6 @@
     take_faces(f0, ysend.at[0])
     faces0 = face_copies(f0, ysend.at[0], yrecv.at[0], gx, gy, fsend.at[0], frecv.at[0])
     pl.semaphore_wait(barrier, NDEV - 1)
-    start_all(faces0)
 
     def block(ref, d):
         return ref.at[pl.ds(pl.multiple_of(d * CAP, CAP), CAP), :]
@@ -320,7 +329,9 @@
         ).start()
         return carry
 
-    lax.fori_loop(1, NDEV, send_rows, 0)
+    lax.fori_loop(1, 40, send_rows, 0)
+    start_all(faces0)
+    lax.fori_loop(40, NDEV, send_rows, 0)
     own_meta = pltpu.make_async_copy(meta_out.at[me], meta_in.at[me], self_sem.at[0])
     own_rows = pltpu.make_async_copy(block(outgoing, me), block(incoming, me), self_sem.at[1])
     own_meta.start()
@@ -384,10 +395,10 @@
     wait_sends(mat_copies)
     wait_recvs(heat_copies)
 
-    solid_step(s0, s1, cond, heat)
-    solid_step(s1, s0, cond, heat)
-    solid_step(s0, s1, cond, heat)
-    solid_step(s1, s0, cond, heat)
+    solid_step(s0, s1, cond, heat, 1)
+    solid_step(s1, s0, cond, heat, 2)
+    solid_step(s0, s1, cond, heat, 3)
+    solid_step(s1, s0, cond, heat, 4)
 
     done = s0[WT : WT + SX, R0 : R0 + SY, :]
     done_b = halves(done.reshape(SLOTS, LN))
@@ -480,7 +491,16 @@
 
 def store(*refs):
     sems = refs[-1]
-    copies = [pltpu.make_async_copy(refs[i], refs[4 + i], sems.at[i]) for i in range(4)]
+    pieces = CX // 2
+    copies = [
+        pltpu.make_async_copy(
+            refs[0].at[pl.ds(2 * i, 2)], refs[4].at[pl.ds(2 * i, 2)], sems.at[i]
+        )
+        for i in range(pieces)
+    ]
+    copies += [
+        pltpu.make_async_copy(refs[i], refs[4 + i], sems.at[pieces + i]) for i in range(1, 4)
+    ]
     for copy in copies:
         copy.start()
     for copy in copies:
@@ -530,7 +550,7 @@
         out_shape=tuple(jax.ShapeDtypeStruct(r.shape, F32) for r in results),
         in_specs=[pl.BlockSpec(memory_space=pl.ANY)] * 4,
         out_specs=(pl.BlockSpec(memory_space=pl.ANY),) * 4,
-        scratch_shapes=[dma((4,))],
+        scratch_shapes=[dma((CX // 2 + 4,))],
         compiler_params=pltpu.CompilerParams(vmem_limit_bytes=1024 * 1024),
     )(*results)
 

time: 81.9 us -> 81.3 us (level)
  no operation moved by 1% of the time
where the time goes in v4:
time: 81.3 us; the launch traced here: 81.2 us
  Pallas kernels  80.5 us (99%)
    pallas_call x1, Pallas kernels, body(): pl.pallas_call(kernel, out_shape=(jax.ShapeDtypeStruct((CX, CY, NT * LN),...  77.9 us
    pallas_call x1, Pallas kernels, body(): pl.pallas_call(store, out_shape=tuple((jax.ShapeDtypeStruct(r.shape, F32)...  2.6 us

profile of v4, /device:TPU:1, one launch (start us, length us, event | category | flops | bytes accessed | tf_op | source)
XLA Modules:
  0.0 81.2 jit_solution(17598660985204943695)
XLA Ops:
  0.6 77.9 %shard_map.111 = (f32[16,64,1024]{2,1,0:T(8,128)S(1)}, f32[1024,128]{1,0:T(8,128)S(1)}, f32[16,32,128]{2,1,0:T(8,128)S(1)}, f32[3,16,32,128]{3,2,1,0:T(8,128)S(1)}) custom-call(f32[16,64,1024]{2,1,0:T(8,128)} %fluid_in.1, bf16[3,16,64,1024]{3,2,1,0:T(8,128)(2,1)} %vel_in.1, f32[16,64,128]{2,1,0:T(8,128)} %wall_in.1, s32[16,64,128]{2,1,0:T(8,128)} %mask_in.1, ...), custom_call_target="tpu_custom_call" | custom-call | tf_op jit(solution)/shard_map/pallas_call | solution.py:516
  78.6 2.6 %shard_map.112 = (f32[16,64,1024]{2,1,0:T(8,128)}, f32[16,64,128]{2,1,0:T(8,128)}, f32[16,32,128]{2,1,0:T(8,128)}, f32[3,16,32,128]{3,2,1,0:T(8,128)}) custom-call(f32[16,64,1024]{2,1,0:T(8,128)S(1)} %get-tuple-element.8.refs_0_, f32[16,64,128]{2,1,0:T(8,128)S(1)} %bitcast.2, f32[16,32,128]{2,1,0:T(8,128)S(1)} %get-tuple-element.10.refs_2_, ...), custom_call_target="tpu_custom_call" | custom-call | tf_op jit(solution)/shard_map/pallas_call | solution.py:548

commit v5 on v4

--- a/solution.py
+++ b/solution.py
@@ -337,25 +337,25 @@
     own_meta.start()
     own_rows.start()
 
+    load_vel.wait()
+    wait_recvs(faces0)
+    put_faces(f0, yrecv.at[0])
+
+    def keep(t, x, h, value):
+        f1[t, x + 1, PADY + 16 * h : PADY + 16 * h + 16, :] = value
+
+    def step_one(x, carry):
+        fluid_plane(f0, keep, vel, flux, x)
+        return carry
+
+    lax.fori_loop(0, CX, step_one, 0)
+
     load_solid.wait()
     load_mat.wait()
     temp_copies = spread_copies(s0, gx, gy, WT, ssend.at[0], srecv.at[0])
     mat_copies = spread_copies(mat, gx, gy, WH, ssend.at[1], srecv.at[1])
     start_all(temp_copies)
     start_all(mat_copies)
-
-    load_vel.wait()
-    wait_recvs(faces0)
-    put_faces(f0, yrecv.at[0])
-
-    def keep(t, x, h, value):
-        f1[t, x + 1, PADY + 16 * h : PADY + 16 * h + 16, :] = value
-
-    def step_one(x, carry):
-        fluid_plane(f0, keep, vel, flux, x)
-        return carry
-
-    lax.fori_loop(0, CX, step_one, 0)
 
     take_faces(f1, ysend.at[1])
     faces1 = face_copies(f1, ysend.at[1], yrecv.at[1], gx, gy, fsend.at[1], frecv.at[1])

time: 81.3 us -> 85.1 us (1.047); the launches traced: 81.2 us -> 83.5 us
  Pallas kernels: 80.5 us -> 82.9 us
    pallas_call x1, Pallas kernels: 77.9 us -> 80.3 us  [body(): pl.pallas_call(kernel, out_shape=(jax.ShapeDtypeStruct((CX, CY, NT * LN),...]
where the time goes in v5:
time: 85.1 us; the launch traced here: 83.5 us
  Pallas kernels  82.9 us (97%)
    pallas_call x1, Pallas kernels, body(): pl.pallas_call(kernel, out_shape=(jax.ShapeDtypeStruct((CX, CY, NT * LN),...  80.3 us
    pallas_call x1, Pallas kernels, body(): pl.pallas_call(store, out_shape=tuple((jax.ShapeDtypeStruct(r.shape, F32)...  2.6 us

profile of v5, /device:TPU:1, one launch (start us, length us, event | category | flops | bytes accessed | tf_op | source)
XLA Modules:
  0.0 83.5 jit_solution(8816892608217269638)
XLA Ops:
  0.6 80.3 %shard_map.111 = (f32[16,64,1024]{2,1,0:T(8,128)S(1)}, f32[1024,128]{1,0:T(8,128)S(1)}, f32[16,32,128]{2,1,0:T(8,128)S(1)}, f32[3,16,32,128]{3,2,1,0:T(8,128)S(1)}) custom-call(f32[16,64,1024]{2,1,0:T(8,128)} %fluid_in.1, bf16[3,16,64,1024]{3,2,1,0:T(8,128)(2,1)} %vel_in.1, f32[16,64,128]{2,1,0:T(8,128)} %wall_in.1, s32[16,64,128]{2,1,0:T(8,128)} %mask_in.1, ...), custom_call_target="tpu_custom_call" | custom-call | tf_op jit(solution)/shard_map/pallas_call | solution.py:516
  80.9 2.6 %shard_map.112 = (f32[16,64,1024]{2,1,0:T(8,128)}, f32[16,64,128]{2,1,0:T(8,128)}, f32[16,32,128]{2,1,0:T(8,128)}, f32[3,16,32,128]{3,2,1,0:T(8,128)}) custom-call(f32[16,64,1024]{2,1,0:T(8,128)S(1)} %get-tuple-element.8.refs_0_, f32[16,64,128]{2,1,0:T(8,128)S(1)} %bitcast.2, f32[16,32,128]{2,1,0:T(8,128)S(1)} %get-tuple-element.10.refs_2_, ...), custom_call_target="tpu_custom_call" | custom-call | tf_op jit(solution)/shard_map/pallas_call | solution.py:548
